TPU v7x, 256 devices: a whole 4x4x8 slice. The times are simulated.
256 devices in a mesh: loop: 16 (over x, z_lo), rep: 16 (over z_hi, y, core).
Axes of the slice: x: 4, y: 4, z: 8 (z_hi: 2, z_lo: 4; z = z_hi * 4 + z_lo), core: 2. Of those that a mesh axis runs over, the one named last changes fastest.
Arguments:
- features: float32 [8192, 128], P('loop'), may hold values from -6 to 6
- weight: float32 [128, 256], replicated, may hold values from -0.5 to 0.5
- bias: float32 [256], replicated, may hold values from -3 to 3
- tile_values: float32 [4096, 128, 128], P(('loop', 'rep')), may hold values from -0.125 to 0.125
- tile_rows: int32 [4096], P(('loop', 'rep')), may hold values from 0 to 63, as said below
- tile_cols: int32 [4096], P(('loop', 'rep')), may hold values from 0 to 63, as said below
- tile_count: int32 [256], P(('loop', 'rep')), may hold values from 1 to 16, as said below
- cotangent: float32 [8192, 256], P('loop'), may hold values from -0.6 to 0.6
Outputs:
- output: float32 [8192, 256], P('loop')
- grad_features: float32 [8192, 128], P('loop')
- grad_weight: float32 [128, 256], replicated
- grad_bias: float32 [256], replicated
Inputs may be any that keep to these rules, and one draw needn't show every extreme that they name: `tile_rows`: every slot of a device at loop index l names a row block from l * 4 to (l + 1) * 4 - 1. `tile_cols`: for every loop index m, the live slots of one device name at most 2 different column blocks from m * 4 to (m + 1) * 4 - 1; for every loop index some device names exactly 2 of one such range. `tile_count`: for every loop index some device has all 16 slots live.
All inputs are finite; a program needn't handle non-finite values.
Results may differ from a plain program's by a relative error of at most 0.0001.
Values sent between devices are 32-bit elements; how exact they have to be, the bound alone decides.
A program may use at most 64 MiB of HBM per device.

v0:
```python
import jax
import jax.numpy as jnp
from jax import lax
from jax.sharding import PartitionSpec as P


def per_device(features, weight, bias, tile_values, tile_rows, tile_cols, tile_count, cotangent):
    highest = lax.Precision.HIGHEST
    tile_side = tile_values.shape[1]
    rows_here = features.shape[0]
    nblocks = rows_here // tile_side
    slots = tile_values.shape[0]
    local_rows = tile_rows - lax.axis_index("loop") * nblocks
    live_slot = (jnp.arange(slots, dtype=jnp.int32) < tile_count[0]).astype(jnp.float32)
    row_pick = (local_rows[:, None] == jnp.arange(nblocks, dtype=jnp.int32)[None, :]).astype(
        jnp.float32
    )
    row_pick = row_pick * live_slot[:, None]
    moved = jnp.dot(features, weight, precision=highest)
    gathered = lax.all_gather(moved, "loop", axis=0, tiled=True)
    width = gathered.shape[1]
    blocks = gathered.reshape(-1, tile_side, width)[tile_cols]
    products = jnp.einsum("kij,kjf->kif", tile_values, blocks, precision=highest)
    summed = lax.psum(
        jnp.einsum("kb,kif->bif", row_pick, products, precision=highest), "rep"
    ).reshape(rows_here, -1)
    preactive = summed + bias
    logistic = jax.nn.sigmoid(preactive)
    output = preactive * logistic
    gradient = cotangent * logistic * (1.0 + preactive * (1.0 - logistic))
    source_blocks = gradient.reshape(nblocks, tile_side, gradient.shape[1])[
        jnp.clip(local_rows, 0, nblocks - 1)
    ]
    outgoing = jnp.einsum("kji,kjf->kif", tile_values, source_blocks, precision=highest)
    outgoing = outgoing * live_slot[:, None, None]
    span = rows_here * lax.axis_size("loop") // tile_side + 2
    column_pick = (tile_cols[:, None] == jnp.arange(span, dtype=jnp.int32)[None, :]).astype(
        jnp.float32
    )
    placed = jnp.einsum("kb,kif->bif", column_pick, outgoing, precision=highest)
    placed = placed.reshape(span * tile_side, outgoing.shape[2])
    term = lax.psum_scatter(
        lax.slice_in_dim(placed, 0, rows_here * lax.axis_size("loop"), axis=0),
        "loop",
        scatter_dimension=0,
        tiled=True,
    )
    own_rows = lax.psum(term, "rep")
    weight_term = jnp.dot(features.T, own_rows, precision=highest)
    grad_rows = jnp.dot(own_rows, weight.T, precision=highest)
    bias_term = jnp.sum(gradient, axis=0)
    grad_weight, grad_bias = lax.psum((weight_term, bias_term), "loop")
    return (output, grad_rows, grad_weight, grad_bias)


def solution(mesh):
    return jax.shard_map(
        per_device,
        mesh=mesh,
        in_specs=(
            P("loop", None),
            P(),
            P(),
            P(("loop", "rep"), None, None),
            P(("loop", "rep")),
            P(("loop", "rep")),
            P(("loop", "rep")),
            P("loop", None),
        ),
        out_specs=(P("loop", None), P("loop", None), P(), P()),
        check_vma=False,
    )
```

profile of v0, /device:TPU:1, one launch (start us, length us, event | category | flops | bytes accessed | tf_op | source)
XLA Modules:
  0.0 944.2 jit_solution(14281771124516442620)
XLA Ops:
  7.2 0.0 copy-start
  7.2 0.0 all-gather.2.cloned.1.call-start
  7.2 2.4 fusion.16
  9.6 0.0 all-gather.2.cloned.1.call-update
  9.7 0.0 all-reduce.4.cloned.1.call-start
  10.4 0.7 compare_select_fusion.1
  11.1 0.7 compare_select_fusion
  11.7 190.0 %all-gather.2.cloned.1.call-done = f32[8192,256]{1,0:T(8,128)} async-done(((f32[512,256]{1,0:T(8,128)}), f32[8192,256]{1,0:T(8,128)}) %all-gather.2.cloned.1.call-update) | async-done | bytes 8388624 | tf_op jit(solution)/shard_map/all_gather | solution.py:20
  201.7 4.1 gather_fusion
  205.8 0.0 copy-done
  205.8 5.1 fusion.17
  210.9 2.2 copy.16
  213.2 0.0 copy-start.4
  213.2 0.0 copy-start.3
  213.2 1.1 fusion.2
  214.3 0.9 copy.13
  215.2 0.0 all-reduce.4.cloned.1.call-update
  215.2 0.0 reduce-scatter.2.cloned.1.call-start
  215.3 0.0 copy-done.4
  215.3 0.1 fusion.7
  215.4 175.6 %all-reduce.4.cloned.1.call-done = f32[512,256]{1,0:T(8,128)} async-done(((f32[512,256]{1,0:T(8,128)}), f32[512,256]{1,0:T(8,128)}) %all-reduce.4.cloned.1.call-update) | async-done | bytes 524304 | tf_op jit(solution)/shard_map/psum | solution.py:24
  391.0 0.0 copy-done.3
  391.0 2.2 fusion.15
  393.2 2.0 gather_fusion.1
  395.2 5.3 fusion.18
  400.6 2.2 copy.17
  402.8 5.2 fusion
  408.0 8.1 copy.14
  416.0 0.0 copy-start.1
  416.1 0.0 copy-start.2
  416.1 0.0 reduce-scatter.2.cloned.1.call-update
  416.1 0.0 all-reduce.6.cloned.1.call-start
  416.1 188.7 %reduce-scatter.2.cloned.1.call-done = f32[512,256]{1,0:T(8,128)} async-done(((f32[8192,256]{1,0:T(8,128)}), f32[512,256]{1,0:T(8,128)}) %reduce-scatter.2.cloned.1.call-update) | async-done | bytes 524304 | tf_op jit(solution)/shard_map/reduce_scatter | solution.py:42
  604.8 0.0 all-reduce.6.cloned.1.call-update
  604.8 0.0 all-reduce.8.cloned.1.call-start
  604.9 32.9 %psum.31 = f32[256]{0:T(256)} all-reduce(f32[256]{0:T(256)S(1)} %get-tuple-element.12), channel_id=1, replica_groups=mesh['loop'=16,'rep'=16] {'loop'}, use_global_device_ids=true, to_apply=%region_5.6 | all-reduce | flops 256 | bytes 2048 | tf_op jit(solution)/shard_map/psum | solution.py:52
  637.7 145.5 %all-reduce.6.cloned.1.call-done = f32[512,256]{1,0:T(8,128)} async-done(((f32[512,256]{1,0:T(8,128)}), f32[512,256]{1,0:T(8,128)}) %all-reduce.6.cloned.1.call-update) | async-done | bytes 524304 | tf_op jit(solution)/shard_map/psum | solution.py:48
  783.3 0.0 copy-done.1
  783.3 2.7 convolution_bitcast_fusion
  786.0 0.0 all-reduce.8.cloned.1.call-update
  786.0 0.0 copy-done.2
  786.0 2.3 fusion.19
  788.3 147.7 %all-reduce.8.cloned.1.call-done = f32[128,256]{0,1:T(8,128)} async-done(((f32[128,256]{0,1:T(8,128)}), f32[128,256]{0,1:T(8,128)}) %all-reduce.8.cloned.1.call-update) | async-done | bytes 131088 | tf_op jit(solution)/shard_map/psum | solution.py:52
  936.0 1.7 copy.15
  (3 shorter events, 0.0 us)
Async XLA Ops:
  7.2 198.7 %copy-start = (f32[16,128,128]{2,1,0:T(8,128)S(1)}, f32[16,128,128]{2,1,0:T(8,128)}, u32[]{:S(2)}) copy-start(f32[16,128,128]{2,1,0:T(8,128)} %param.11) | copy-start | bytes 3145732
  7.2 194.6 %all-gather.2.cloned.1.call-start = ((), (), s32[]{:S(2)}) async-start(), calls=%async_computation.1 | async-start | bytes 8912896 | tf_op jit(solution)/shard_map/all_gather | solution.py:20
  9.7 381.3 %all-reduce.4.cloned.1.call-start = ((), (), s32[]{:S(2)}) async-start(), calls=%async_computation.2 | async-start | bytes 1048576 | tf_op jit(solution)/shard_map/psum | solution.py:24
  213.2 2.1 copy-start.4
  213.2 177.8 %copy-start.3 = (f32[256]{0:T(256)S(1)}, f32[256]{0:T(256)}, u32[]{:S(2)}) copy-start(f32[256]{0:T(256)} %param.10) | copy-start | bytes 3076
  215.2 389.6 %reduce-scatter.2.cloned.1.call-start = ((), (), s32[]{:S(2)}) async-start(), calls=%async_computation.3 | async-start | bytes 8912896 | tf_op jit(solution)/shard_map/reduce_scatter | solution.py:42
  416.0 367.2 %copy-start.1 = (f32[512,128]{1,0:T(8,128)S(1)}, f32[512,128]{1,0:T(8,128)}, u32[]{:S(2)}) copy-start(f32[512,128]{1,0:T(8,128)} %param.8) | copy-start | bytes 786436
  416.1 369.9 %copy-start.2 = (f32[128,256]{1,0:T(8,128)S(1)}, f32[128,256]{1,0:T(8,128)}, u32[]{:S(2)}) copy-start(f32[128,256]{1,0:T(8,128)} %param.9) | copy-start | bytes 393220
  416.1 367.2 %all-reduce.6.cloned.1.call-start = ((), (), s32[]{:S(2)}) async-start(), calls=%async_computation.4 | async-start | bytes 1048576 | tf_op jit(solution)/shard_map/psum | solution.py:48
  604.8 331.2 %all-reduce.8.cloned.1.call-start = ((), (), s32[]{:S(2)}) async-start(), calls=%async_computation.5 | async-start | bytes 262144 | tf_op jit(solution)/shard_map/psum | solution.py:52
Sparse Core Ops, SparseCore 0:
  10.4 191.3 all-gather.1
  215.3 175.6 all-reduce.3
  416.2 188.5 reduce-scatter.1
  607.5 175.7 all-reduce.5
  786.3 149.7 all-reduce.7
where the time goes:
time: 954 us; the launch traced here: 944 us
  waiting for transfers between devices  848 us (89%)
  blocking collectives  32.9 us (3%)
  matrix products  24.1 us (3%)
  local copies, waits for them, and re-layouts  21.2 us (2%)
  between operations  14.5 us (2%)
    all_gather x1, waiting for transfers between devices, per_device(): gathered = lax.all_gather(moved, 'loop', axis=0, tiled=True)  190 us
    reduce_scatter x1, waiting for transfers between devices, per_device(): lax.psum_scatter(lax.slice_in_dim(placed, 0, rows_here * lax.axis_size('l...  189 us
    psum x1, waiting for transfers between devices, per_device(): lax.psum(jnp.einsum('kb,kif->bif', row_pick, products, precision=highest)...  176 us
    psum x1, waiting for transfers between devices, per_device(): grad_weight, grad_bias = lax.psum((weight_term, bias_term), 'loop')  148 us
    psum x1, waiting for transfers between devices, per_device(): own_rows = lax.psum(term, 'rep')  146 us
    psum x1, blocking collectives, per_device(): grad_weight, grad_bias = lax.psum((weight_term, bias_term), 'loop')  32.9 us
  transfers between devices with their start and end apart: 5, of which 5 were waited for; matrix products, arithmetic and copies ran while one was open for 0% of the time, Pallas kernels for 0%

commit v1 on v0

v1 whole, which is shorter than its diff:
```python
import jax
import jax.numpy as jnp
from jax import lax
from jax.experimental import pallas as pl
from jax.experimental.pallas import tpu as pltpu
from jax.sharding import PartitionSpec as P

F32, BF16 = jnp.float32, jnp.bfloat16
ROWS_LAST = (((1,), (0,)), ((), ()))
BOTH_LAST = (((1,), (1,)), ((), ()))


def split(v):
    high = v.astype(BF16)
    return high, (v - high.astype(F32)).astype(BF16)


def dot3(a, b, dims=ROWS_LAST):
    def one(p, q):
        return lax.dot_general(p, q, dims, preferred_element_type=F32)

    return one(a[0], b[0]) + (one(a[0], b[1]) + one(a[1], b[0]))


def kernel(
    table_smem, table_any, features, weight, bias, tiles, cotangent,
    out, grad_features, grad_weight, grad_bias,
    sib_table, table_in, feat, tile, t_hi, t_lo, tt_hi, tt_lo,
    agg_part, y_in2, z_out2, z_in2, agg, out_stage, grad, s_hi, s_lo, chain,
    b1, b1_in, b2, b2_in, a1, a1_in, a2, a2_in, line, fin,
    gw, w_out, x_in5, z_out5, z_in5, y_in4, z_out4, z_in4, pay,
    local_sem, send_sem, recv_sem,
):
    loop, rep = lax.axis_index("loop"), lax.axis_index("rep")
    x, zl = lax.div(loop, 4), lax.rem(loop, 4)
    zh, y, c = lax.div(rep, 8), lax.rem(lax.div(rep, 2), 4), lax.rem(rep, 2)
    z = zh * 4 + zl

    def device(xx, yy, zz, cc):
        return {
            "loop": xx * 4 + lax.rem(zz, 4),
            "rep": lax.div(zz, 4) * 8 + yy * 2 + cc,
        }

    def at_x(d):
        return device(lax.rem(x + d + 4, 4), y, z, c)

    def at_y(d):
        return device(x, lax.rem(y + d + 4, 4), z, c)

    def at_z(d):
        return device(x, y, lax.rem(z + d + 8, 8), c)

    def along_a(d):
        return device(
            lax.rem(x + (1 - c) * d + 4, 4), y, lax.rem(z + c * d + 8, 8), c
        )

    def along_b(d):
        return device(
            lax.rem(x + c * d + 4, 4), y, lax.rem(z + (1 - c) * d + 8, 8), c
        )

    sibling = device(x, y, z, 1 - c)
    a, b = (1 - c) * x + c * zl, c * x + (1 - c) * zl

    def chunk(da, db):
        aa, bb = lax.rem(a + da + 4, 4), lax.rem(b + db + 4, 4)
        return c * 32 + (aa * (4 - 3 * c) + bb * (1 + 3 * c)) * 2

    counter = [0]
    sent = []

    def push(src, dst, to, recv=None):
        n = counter[0]
        counter[0] += 1
        copy = pltpu.make_async_remote_copy(
            src_ref=src,
            dst_ref=dst,
            send_sem=send_sem.at[n],
            recv_sem=recv_sem.at[n if recv is None else recv],
            device_id=to,
            device_id_type=pl.DeviceIdType.MESH,
        )
        copy.start()
        sent.append(copy)
        return copy

    own = [
        pltpu.make_async_copy(
            features.at[pl.ds(2 * h, 2)],
            feat.at[pl.ds(32 * h + 2 * loop, 2)],
            local_sem.at[h],
        )
        for h in range(2)
    ]
    for copy in own:
        copy.start()
    tiles_in = pltpu.make_async_copy(tiles, tile.at[pl.ds(0, 16)], local_sem.at[2])
    tiles_in.start()

    partners = [at_x(1), at_x(2), at_x(3), at_y(1), at_y(2), at_y(3)]
    partners += [at_z(1), at_z(2), at_z(4), at_z(6), at_z(7), sibling]
    barrier = pltpu.get_barrier_semaphore()
    for partner in partners:
        pl.semaphore_signal(
            barrier, inc=1, device_id=partner, device_id_type=pl.DeviceIdType.MESH
        )
    pl.semaphore_wait(barrier, len(partners))

    for copy in own:
        copy.wait()

    def block_pair(da, db):
        return feat.at[pl.ds(chunk(da, db), 2)]

    def one_block(da, db, j):
        return feat.at[pl.ds(chunk(da, db) + j, 1)]

    sib_chunks = 90

    def to_sibling(da, db):
        push(block_pair(da, db), block_pair(da, db), sibling, recv=sib_chunks)

    a_right = push(block_pair(0, 0), block_pair(0, 0), along_a(1))
    a_left = push(block_pair(0, 0), block_pair(0, 0), along_a(-1))
    b_right, b_left, b_fwd = {}, {}, {}

    def out_b(da):
        b_right[da] = push(block_pair(da, 0), block_pair(da, 0), along_b(1))
        b_left[da] = push(block_pair(da, 0), block_pair(da, 0), along_b(-1))

    def relay_b(da):
        b_right[da].wait_recv()
        first = push(one_block(da, -1, 0), one_block(da, -1, 0), along_b(1))
        to_sibling(da, -1)
        b_left[da].wait_recv()
        second = push(one_block(da, 1, 1), one_block(da, 1, 1), along_b(-1))
        to_sibling(da, 1)
        b_fwd[da] = (first, second)

    out_b(0)
    table_move = push(table_any, table_in, sibling)
    tiles_move = push(tiles, tile.at[pl.ds(16, 16)], sibling)

    tiles_in.wait()

    def split_tile(s):
        t_hi[s], t_lo[s] = split(tile[s])
        tt_hi[s], tt_lo[s] = split(tile[s].T)

    def split_tiles(start):
        def two(s, _):
            split_tile(start + 2 * s)
            split_tile(start + 2 * s + 1)
            return 0

        lax.fori_loop(0, 8, two, 0)

    a_right.wait_recv()
    a_fwd_right = push(one_block(-1, 0, 0), one_block(-1, 0, 0), along_a(1))
    out_b(-1)
    to_sibling(-1, 0)
    a_left.wait_recv()
    a_fwd_left = push(one_block(1, 0, 1), one_block(1, 0, 1), along_a(-1))
    out_b(1)
    to_sibling(1, 0)
    split_tiles(0)
    relay_b(0)
    a_fwd_right.wait_recv()
    a_fwd_left.wait_recv()
    out_b(2)
    to_sibling(2, 0)
    table_move.wait_recv()
    table_local = pltpu.make_async_copy(table_in, sib_table, local_sem.at[3])
    table_local.start()
    tiles_move.wait_recv()
    split_tiles(16)
    table_local.wait()
    for da in (-1, 1, 2):
        relay_b(da)
    for da in (0, -1, 1, 2):
        b_fwd[da][0].wait_recv()
        b_fwd[da][1].wait_recv()
        to_sibling(da, 2)
    pltpu.make_async_copy(
        feat.at[pl.ds(0, 30)], feat.at[pl.ds(0, 30)], recv_sem.at[sib_chunks]
    ).wait()

    agg_part[...] = jnp.zeros_like(agg_part)
    for side, table in enumerate((table_smem, sib_table)):

        def add_products(step, _, side=side, table=table):
            for u in range(4):
                s = step * 4 + u
                block = split(feat[table[0, s]])
                product = dot3((t_hi[16 * side + s], t_lo[16 * side + s]), block)
                row = table[0, 16 + s]
                for j in range(2):
                    keep = (row == 2 * c + j).astype(F32)
                    agg_part[128 * j : 128 * j + 128, :] += product * keep
            return 0

        lax.fori_loop(0, 4, add_products, 0)

    def reduce_rep(part, y_in, z_out, z_in):
        moves = []
        for d in (2, 1, 3):
            there = lax.rem(y + d, 4)
            moves.append(
                push(part.at[pl.ds(there * 64, 64)], y_in.at[y], at_y(d))
            )
        y_in[y] = part[pl.ds(pl.multiple_of(y * 64, 64), 64), :]
        for move in moves:
            move.wait_recv()
        z_out[...] = (y_in[0] + y_in[1]) + (y_in[2] + y_in[3])
        swap = push(z_out, z_in, at_z(4))
        swap.wait_recv()
        return z_out[...] + z_in[...]

    def gather_rep(buf, sem, whole):
        mine = buf.at[c * 4 + y]
        moves = [(d, push(mine, mine, at_y(d))) for d in (2, 1, 3)]
        push(mine, mine, sibling, recv=sem)
        for d, move in (moves[1], moves[2], moves[0]):
            move.wait_recv()
            got = buf.at[c * 4 + lax.rem(y - d + 4, 4)]
            push(got, got, sibling, recv=sem)
        pltpu.make_async_copy(
            buf.at[pl.ds(0, 4)], buf.at[pl.ds(0, 4)], recv_sem.at[sem]
        ).wait()

    total = reduce_rep(agg_part, y_in2, z_out2, z_in2)
    agg[c * 4 + y] = total
    gather_rep(agg, 91, None)

    weights = split(weight[...])
    for r in range(4):
        rows = slice(128 * r, 128 * r + 128)
        mine = agg[2 * r : 2 * r + 2].reshape(128, 128)
        pre = dot3(split(mine), weights) + bias[...]
        logistic = 1.0 / (1.0 + jnp.exp(-pre))
        out_stage[rows, :] = pre * logistic
        g = cotangent[rows, :] * logistic * (1.0 + pre * (1.0 - logistic))
        grad[rows, :] = g
        s_hi[r], s_lo[r] = split(dot3(split(g), weights, BOTH_LAST))
    out_move = pltpu.make_async_copy(out_stage, out, local_sem.at[4])
    out_move.start()

    chain[16] = jnp.zeros((128, 128), F32)
    chain[33] = jnp.zeros((128, 128), F32)
    for side, table in enumerate((table_smem, sib_table)):

        def add_transposed(step, _, side=side, table=table):
            for u in range(4):
                s = step * 4 + u
                row = table[0, 32 + s]
                product = dot3(
                    (tt_hi[16 * side + s], tt_lo[16 * side + s]),
                    (s_hi[row], s_lo[row]),
                )
                chain[17 * side + s] = product + chain[17 * side + table[0, 48 + s]]
            return 0

        lax.fori_loop(0, 4, add_transposed, 0)

    def dense(da, db, j):
        f = chunk(da, db) + j
        return chain[table_smem[0, 64 + f]] + chain[17 + sib_table[0, 64 + f]]

    order = (2, -1, 1, 0)
    to1 = {}
    for k, da in enumerate(order):
        b1[0, k] = dense(da, 2, 0)
        b1[1, k] = dense(da, 2, 1)
        to1[k] = (
            push(b1.at[0, k], b1_in.at[0, k], along_b(1)),
            push(b1.at[1, k], b1_in.at[1, k], along_b(-1)),
        )

    gw[...] = dot3(
        split(agg[...].reshape(512, 128).T), split(grad[...])
    )
    w_out[0:16, :] = gw[pl.ds(pl.multiple_of((c * 4 + y) * 16, 16), 16), :]
    w_out[16:24, :] = jnp.broadcast_to(
        jnp.sum(grad[...], axis=0, keepdims=True), (8, 256)
    )
    x_in5[x] = w_out[...]

    to2 = {}
    for k, da in enumerate(order):
        for i, d in ((0, 1), (1, -1)):
            b2[i, k, 1 - i] = dense(da, d, 1 - i)
            to1[k][i].wait_recv()
            b2[i, k, i] = dense(da, d, i) + b1_in[i, k]
            to2[k, i] = push(b2.at[i, k], b2_in.at[i, k], along_b(d))
    x_moves = [push(w_out, x_in5.at[x], at_x(d)) for d in (2, 1, 3)]
    for move in x_moves:
        move.wait_recv()
    z_out5[...] = (x_in5[0] + x_in5[1]) + (x_in5[2] + x_in5[3])
    z_in5[zl] = z_out5[...]
    z_moves = [push(z_out5, z_in5.at[zl], at_z(d)) for d in (2, 1, -1)]

    to3, to4 = {}, {}
    for k, da in enumerate(order):
        for j in range(2):
            line[k, j] = dense(da, 0, j)
        for i in range(2):
            to2[k, i].wait_recv()
        for j in range(2):
            line[k, j] += b2_in[0, k, j] + b2_in[1, k, j]
        if da == 2:
            to3 = (
                push(line.at[k, 0], a1_in.at[0], along_a(1)),
                push(line.at[k, 1], a1_in.at[1], along_a(-1)),
            )
        elif da != 0:
            i = 0 if da == 1 else 1
            to3[i].wait_recv()
            line[k, i] += a1_in[i]
            to4[i] = push(line.at[k], a2_in.at[i], along_a(da))
        else:
            to4[0].wait_recv()
            to4[1].wait_recv()
            for j in range(2):
                fin[128 * j : 128 * j + 128, :] = line[k, j] + (
                    a2_in[0, j] + a2_in[1, j]
                )
    for move in z_moves:
        move.wait_recv()
    total = reduce_rep(fin, y_in4, z_out4, z_in4)
    here = c * 4 + y
    pay[here, 0:64, :] = total
    summed = (z_in5[0] + z_in5[1]) + (z_in5[2] + z_in5[3])
    pay[here, 64:80, :] = summed[0:16, 0:128]
    pay[here, 80:96, :] = summed[0:16, 128:256]
    grad_bias[...] = summed[16:24, :]
    gather_rep(pay, 92, None)
    for i in range(8):
        grad_features[64 * i : 64 * i + 64, :] = pay[i, 0:64, :]
        grad_weight[16 * i : 16 * i + 16, 0:128] = pay[i, 64:80, :]
        grad_weight[16 * i : 16 * i + 16, 128:256] = pay[i, 80:96, :]
    out_move.wait()
    for copy in sent:
        copy.wait_send()


def make_table(tile_rows, tile_cols, tile_count):
    slots = tile_cols.shape[0]
    ids = jnp.arange(slots, dtype=jnp.int32)
    live = ids < tile_count[0]
    spot = lax.rem(lax.div(tile_cols, 2), 2) * 32 + lax.div(tile_cols, 4) * 2
    spot = spot + lax.rem(tile_cols, 2)
    row = lax.rem(tile_rows, 4)
    earlier = (spot[None, :] == spot[:, None]) & live[None, :]
    earlier = earlier & (ids[None, :] < ids[:, None])
    before = jnp.max(jnp.where(earlier, ids[None, :], -1), axis=1)
    blocks = jnp.arange(64, dtype=jnp.int32)
    match = (spot[None, :] == blocks[:, None]) & live[None, :]
    last = jnp.max(jnp.where(match, ids[None, :], -1), axis=1)
    none = slots
    return jnp.concatenate(
        [
            spot,
            jnp.where(live, row, -1),
            row,
            jnp.where(before < 0, none, before),
            jnp.where(last < 0, none, last),
        ]
    )[None, :]


def per_device(features, weight, bias, tile_values, tile_rows, tile_cols, tile_count, cotangent):
    table = make_table(tile_rows, tile_cols, tile_count)
    vmem, anywhere = pltpu.VMEM, pl.BlockSpec(memory_space=pl.ANY)
    in_vmem = pl.BlockSpec(memory_space=pltpu.VMEM)
    square = (128, 128)
    outs = pl.pallas_call(
        kernel,
        out_shape=(
            jax.ShapeDtypeStruct((512, 256), F32),
            jax.ShapeDtypeStruct((512, 128), F32),
            jax.ShapeDtypeStruct((128, 256), F32),
            jax.ShapeDtypeStruct((8, 256), F32),
        ),
        in_specs=[
            pl.BlockSpec(memory_space=pltpu.SMEM),
            anywhere,
            anywhere,
            in_vmem,
            in_vmem,
            anywhere,
            in_vmem,
        ],
        out_specs=(anywhere, in_vmem, in_vmem, in_vmem),
        scratch_shapes=[
            pltpu.SMEM((1, 128), jnp.int32),
            vmem((1, 128), jnp.int32),
            vmem((64, *square), F32),
            vmem((32, *square), F32),
            vmem((32, *square), BF16),
            vmem((32, *square), BF16),
            vmem((32, *square), BF16),
            vmem((32, *square), BF16),
            vmem((256, 128), F32),
            vmem((4, 64, 128), F32),
            vmem((64, 128), F32),
            vmem((64, 128), F32),
            vmem((8, 64, 128), F32),
            vmem((512, 256), F32),
            vmem((512, 256), F32),
            vmem((4, *square), BF16),
            vmem((4, *square), BF16),
            vmem((34, *square), F32),
            vmem((2, 4, *square), F32),
            vmem((2, 4, *square), F32),
            vmem((2, 4, 2, *square), F32),
            vmem((2, 4, 2, *square), F32),
            vmem((8, 128), F32),
            vmem((2, *square), F32),
            vmem((8, 128), F32),
            vmem((2, 2, *square), F32),
            vmem((4, 2, *square), F32),
            vmem((256, 128), F32),
            vmem((128, 256), F32),
            vmem((24, 256), F32),
            vmem((4, 24, 256), F32),
            vmem((24, 256), F32),
            vmem((4, 24, 256), F32),
            vmem((4, 64, 128), F32),
            vmem((64, 128), F32),
            vmem((64, 128), F32),
            vmem((8, 96, 128), F32),
            pltpu.SemaphoreType.DMA((5,)),
            pltpu.SemaphoreType.DMA((96,)),
            pltpu.SemaphoreType.DMA((96,)),
        ],
        compiler_params=pltpu.CompilerParams(
            collective_id=0, has_side_effects=True, vmem_limit_bytes=40 * 1024 * 1024
        ),
        cost_estimate=pl.CostEstimate(
            flops=400_000_000, bytes_accessed=4_000_000, transcendentals=131072
        ),
    )(
        table,
        table,
        features.reshape(4, *square),
        weight,
        bias[None, :],
        tile_values,
        cotangent,
    )
    output, grad_features, grad_weight, grad_bias = outs
    return output, grad_features, grad_weight, grad_bias[0]


def solution(mesh):
    return jax.shard_map(
        per_device,
        mesh=mesh,
        in_specs=(
            P("loop", None),
            P(),
            P(),
            P(("loop", "rep"), None, None),
            P(("loop", "rep")),
            P(("loop", "rep")),
            P(("loop", "rep")),
            P("loop", None),
        ),
        out_specs=(P("loop", None), P("loop", None), P(), P()),
        check_vma=False,
    )
```

time: 954 us -> 92.5 us (0.10)
  waiting for transfers between devices: 848 us -> 0 us
  Pallas kernels: 0 us -> 81.7 us
  blocking collectives: 32.9 us -> 0 us
  matrix products: 24.1 us -> 0 us
  between operations: 14.5 us -> 1.32 us
  local copies, waits for them, and re-layouts: 21.2 us -> 8.88 us
    psum x3 -> x0, waiting for transfers between devices: 469 us -> none  [the longest x1 176 us: per_device(): lax.psum(jnp.einsum('kb,kif->bif', row_pick, products, precision=highest)...]
    all_gather x1 -> x0, waiting for transfers between devices: 190 us -> none  [per_device(): gathered = lax.all_gather(moved, 'loop', axis=0, tiled=True)]
    reduce_scatter x1 -> x0, waiting for transfers between devices: 189 us -> none  [per_device(): lax.psum_scatter(lax.slice_in_dim(placed, 0, rows_here * lax.axis_size('l...]
    pallas_call x0 -> x1, Pallas kernels: none -> 81.7 us  [per_device(): pl.pallas_call(kernel, out_shape=(jax.ShapeDtypeStruct((512, 256), F32),...]
    psum x1 -> x0, blocking collectives: 32.9 us -> none  [per_device(): grad_weight, grad_bias = lax.psum((weight_term, bias_term), 'loop')]
    dot_general x7 -> x0, matrix products: 24.1 us -> none  [the longest x1 5.32 us: per_device(): jnp.einsum('kji,kjf->kif', tile_values, source_blocks, precision=highest)]
  transfers between devices with their start and end apart: 5 -> 0, of which waited for: 5 -> 0; matrix products, arithmetic and copies ran while one was open for 0% -> 0% of each run, Pallas kernels for 0% -> 0%
where the time goes in v1:
time: 92.5 us; the launch traced here: 92.2 us
  Pallas kernels  81.7 us (88%)
  local copies, waits for them, and re-layouts  8.88 us (10%)
  between operations  1.32 us (1%)
    pallas_call x1, Pallas kernels, per_device(): pl.pallas_call(kernel, out_shape=(jax.ShapeDtypeStruct((512, 256), F32),...  81.7 us
    unnamed x17, local copies, waits for them, and re-layouts  8.23 us

profile of v1, /device:TPU:1, one launch (start us, length us, event | category | flops | bytes accessed | tf_op | source)
XLA Modules:
  0.0 92.2 jit_solution(9274273188684925099)
XLA Ops:
  1.3 0.0 copy-start.6
  1.3 0.6 copy-done.6
  2.0 0.2 select_reduce_fusion.1
  2.1 0.1 select_reduce_fusion
  2.2 0.0 copy-start.5
  2.3 0.6 copy-done.5
  2.9 0.1 concatenate.3
  3.0 0.0 copy-start.4
  3.0 0.7 copy-done.4
  3.7 0.0 copy-start
  3.7 1.2 %copy-done = f32[16,128,128]{2,1,0:T(8,128)S(1)} copy-done((f32[16,128,128]{2,1,0:T(8,128)S(1)}, f32[16,128,128]{2,1,0:T(8,128)}, u32[]{:S(2)}) %copy-start) | copy-done | bytes 1048600
  4.9 0.0 copy-start.1
  4.9 1.0 %copy-done.1 = f32[512,256]{1,0:T(8,128)S(1)} copy-done((f32[512,256]{1,0:T(8,128)S(1)}, f32[512,256]{1,0:T(8,128)}, u32[]{:S(2)}) %copy-start.1) | copy-done | bytes 524312
  5.9 0.0 copy-start.2
  5.9 0.9 %copy-done.2 = f32[512,128]{1,0:T(8,128)S(1)} copy-done((f32[512,128]{1,0:T(8,128)S(1)}, f32[512,128]{1,0:T(8,128)}, u32[]{:S(2)}) %copy-start.2) | copy-done | bytes 262168
  6.9 0.0 copy-start.3
  6.9 0.9 copy-done.3
  7.8 81.7 %shard_map.118 = (f32[512,256]{1,0:T(8,128)S(1)}, f32[512,128]{1,0:T(8,128)S(1)}, f32[128,256]{1,0:T(8,128)S(1)}, f32[8,256]{1,0:T(8,128)S(1)}) custom-call(s32[1,128]{1,0:T(1,128)S(1)} %bitcast.8, s32[1,128]{1,0:T(1,128)S(1)} %bitcast.9, f32[4,128,128]{2,1,0:T(8,128)S(1)} %bitcast.7, f32[128,256]{1,0:T(8,128)S(1)} %copy-done.3, f32[1,256]{1,0:T(1,128)S(1)} %bitcast.10, ...), custom_call_target="tpu_custom_call" | custom-call | flops 400000000 | bytes 4000000 | tf_op jit(solution)/shard_map/pallas_call | solution.py:378
  89.5 0.6 slice.3
  90.1 0.8 copy.16
  90.9 0.7 copy.17
  91.6 0.7 copy.18
  (4 shorter events, 0.0 us)
Async XLA Ops:
  1.3 0.7 copy-start.6
  2.2 0.7 copy-start.5
  3.0 0.7 copy-start.4
  3.7 1.2 %copy-start = (f32[16,128,128]{2,1,0:T(8,128)S(1)}, f32[16,128,128]{2,1,0:T(8,128)}, u32[]{:S(2)}) copy-start(f32[16,128,128]{2,1,0:T(8,128)} %tiles.1) | copy-start | bytes 3145732
  4.9 1.0 %copy-start.1 = (f32[512,256]{1,0:T(8,128)S(1)}, f32[512,256]{1,0:T(8,128)}, u32[]{:S(2)}) copy-start(f32[512,256]{1,0:T(8,128)} %cotangent.1) | copy-start | bytes 1572868
  5.9 0.9 %copy-start.2 = (f32[512,128]{1,0:T(8,128)S(1)}, f32[512,128]{1,0:T(8,128)}, u32[]{:S(2)}) copy-start(f32[512,128]{1,0:T(8,128)} %param.8) | copy-start | bytes 786436
  6.9 0.9 copy-start.3

commit v2 on v1

v2 whole, which is shorter than its diff:
```python
import jax
import jax.numpy as jnp
from jax import lax
from jax.experimental import pallas as pl
from jax.experimental.pallas import tpu as pltpu
from jax.sharding import PartitionSpec as P

F32, BF16 = jnp.float32, jnp.bfloat16


def split(v):
    high = v.astype(BF16)
    return high, (v - high.astype(F32)).astype(BF16)


def left(v):
    high, low = split(v)
    return jnp.concatenate([high, high, low], axis=1)


def right(v):
    high, low = split(v)
    return jnp.concatenate([high, low, high], axis=0)


def dot(a, b):
    return lax.dot_general(a, b, (((1,), (0,)), ((), ())), preferred_element_type=F32)


def kernel(
    tile_rows, tile_cols, tile_count, features, weight_in, bias_in, tiles, cotangent_in,
    out, grad_features, grad_weight, grad_bias,
    table_out, table_in, own_table, sib_table, feat, tile, weight, bias, cotangent,
    t_left, tt_left, w_right, wt_right,
    agg_part, y_in2, z_out2, z_in2, agg, out_stage, grad, s_right, chain,
    b_out, b_far, b_in, b_far_in, a_in, a_far_in, line, fin,
    gw, w_out, x_in5, z_out5, z_in5, y_in4, z_out4, z_in4, pay,
    local_sem, send_sem, recv_sem,
):
    loop, rep = lax.axis_index("loop"), lax.axis_index("rep")
    x, zl = lax.div(loop, 4), lax.rem(loop, 4)
    zh, y, c = lax.div(rep, 8), lax.rem(lax.div(rep, 2), 4), lax.rem(rep, 2)
    z = zh * 4 + zl

    def device(xx, yy, zz, cc):
        return {
            "loop": xx * 4 + lax.rem(zz, 4),
            "rep": lax.div(zz, 4) * 8 + yy * 2 + cc,
        }

    def at_x(d):
        return device(lax.rem(x + d + 4, 4), y, z, c)

    def at_y(d):
        return device(x, lax.rem(y + d + 4, 4), z, c)

    def at_z(d):
        return device(x, y, lax.rem(z + d + 8, 8), c)

    def along_a(d):
        return device(
            lax.rem(x + (1 - c) * d + 4, 4), y, lax.rem(z + c * d + 8, 8), c
        )

    def along_b(d):
        return device(
            lax.rem(x + c * d + 4, 4), y, lax.rem(z + (1 - c) * d + 8, 8), c
        )

    sibling = device(x, y, z, 1 - c)
    a, b = (1 - c) * x + c * zl, c * x + (1 - c) * zl

    def chunk(da, db):
        aa, bb = lax.rem(a + da + 4, 4), lax.rem(b + db + 4, 4)
        return c * 32 + (aa * (4 - 3 * c) + bb * (1 + 3 * c)) * 2

    counter = [0]
    sent = []

    def push(src, dst, to, recv=None):
        n = counter[0]
        counter[0] += 1
        copy = pltpu.make_async_remote_copy(
            src_ref=src,
            dst_ref=dst,
            send_sem=send_sem.at[n],
            recv_sem=recv_sem.at[n if recv is None else recv],
            device_id=to,
            device_id_type=pl.DeviceIdType.MESH,
        )
        copy.start()
        sent.append(copy)
        return copy

    own = [
        pltpu.make_async_copy(
            features.at[pl.ds(2 * h, 2)],
            feat.at[pl.ds(32 * h + 2 * loop, 2)],
            local_sem.at[h],
        )
        for h in range(2)
    ]
    for copy in own:
        copy.start()
    tiles_in = pltpu.make_async_copy(tiles, tile.at[pl.ds(0, 16)], local_sem.at[2])
    tiles_in.start()
    layer_in = [
        pltpu.make_async_copy(src, dst, local_sem.at[5 + n])
        for n, (src, dst) in enumerate(
            ((weight_in, weight), (bias_in, bias), (cotangent_in, cotangent))
        )
    ]
    for copy in layer_in:
        copy.start()

    partners = [at_x(1), at_x(2), at_x(3), at_y(1), at_y(2), at_y(3)]
    partners += [at_z(1), at_z(2), at_z(6), at_z(7), sibling]
    barrier = pltpu.get_barrier_semaphore()
    for partner in partners:
        pl.semaphore_signal(
            barrier, inc=1, device_id=partner, device_id_type=pl.DeviceIdType.MESH
        )

    table_out[...] = make_table(tile_rows, tile_cols, tile_count)
    table_local = pltpu.make_async_copy(table_out, own_table, local_sem.at[8])
    table_local.start()
    for copy in own:
        copy.wait()
    pl.semaphore_wait(barrier, len(partners))

    def block_pair(da, db):
        return feat.at[pl.ds(chunk(da, db), 2)]

    def one_block(da, db, j):
        return feat.at[pl.ds(chunk(da, db) + j, 1)]

    sib_chunks = 90

    def to_sibling(da, db):
        push(block_pair(da, db), block_pair(da, db), sibling, recv=sib_chunks)

    relayed = (0, -1, 1)
    a_near = [push(block_pair(0, 0), block_pair(0, 0), along_a(d)) for d in (1, -1)]
    b_near, b_two = {}, {}

    def far(src, along):
        return [push(src.at[pl.ds(j, 1)], src.at[pl.ds(j, 1)], along(4 * j - 2)) for j in range(2)]

    def out_b(da):
        b_near[da] = [
            push(block_pair(da, 0), block_pair(da, 0), along_b(d)) for d in (1, -1)
        ]
        if da not in relayed:
            b_two[da] = far(block_pair(da, 0), along_b)

    def near_b(da):
        for i, d in ((0, 1), (1, -1)):
            b_near[da][i].wait_recv()
            if da in relayed:
                view = one_block(da, -d, i)
                b_two.setdefault(da, []).append(push(view, view, along_b(d)))
            to_sibling(da, -d)

    out_b(0)
    a_far = far(block_pair(0, 0), along_a)
    table_move = push(table_out, table_in, sibling)
    tiles_move = push(tiles, tile.at[pl.ds(16, 16)], sibling)

    def split_tiles(start):
        def two(n, _):
            for s in (start + 2 * n, start + 2 * n + 1):
                t_left[s] = left(tile[s])
                tt_left[s] = left(tile[s].T)
            return 0

        lax.fori_loop(0, 8, two, 0)

    for i, d in ((0, 1), (1, -1)):
        a_near[i].wait_recv()
        out_b(-d)
    to_sibling(-1, 0)
    to_sibling(1, 0)
    for move in a_far:
        move.wait_recv()
    out_b(2)
    to_sibling(2, 0)
    near_b(0)
    table_local.wait()
    table_move.wait_recv()
    table_local = pltpu.make_async_copy(table_in, sib_table, local_sem.at[3])
    table_local.start()
    tiles_in.wait()
    split_tiles(0)
    near_b(-1)
    near_b(1)
    tiles_move.wait_recv()
    split_tiles(16)
    for copy in layer_in:
        copy.wait()
    w_right[...] = right(weight[...])
    wt_right[...] = right(weight[...].T)
    table_local.wait()
    near_b(2)
    for da in (0, -1, 1, 2):
        for j in range(2):
            b_two[da][j].wait_recv()
            view = one_block(da, 2, j)
            push(view, view, sibling, recv=sib_chunks)
    pltpu.make_async_copy(
        feat.at[pl.ds(0, 30)], feat.at[pl.ds(0, 30)], recv_sem.at[sib_chunks]
    ).wait()

    agg_part[...] = jnp.zeros_like(agg_part)
    for side, table in enumerate((own_table, sib_table)):

        def add_products(step, _, side=side, table=table):
            for u in range(4):
                s = step * 4 + u
                product = dot(t_left[16 * side + s], right(feat[table[0, s]]))
                row = table[0, 16 + s]
                for j in range(2):
                    keep = (row == 2 * c + j).astype(F32)
                    agg_part[128 * j : 128 * j + 128, :] += product * keep
            return 0

        lax.fori_loop(0, 4, add_products, 0)

    def reduce_rep(part, y_in, z_out, z_in):
        moves = []
        for d in (2, 1, 3):
            there = lax.rem(y + d, 4)
            moves.append(
                push(part.at[pl.ds(there * 64, 64)], y_in.at[y], at_y(d))
            )
        y_in[y] = part[pl.ds(pl.multiple_of(y * 64, 64), 64), :]
        for move in moves:
            move.wait_recv()
        z_out[...] = (y_in[0] + y_in[1]) + (y_in[2] + y_in[3])
        swap = push(z_out, z_in, at_z(4))
        swap.wait_recv()
        return z_out[...] + z_in[...]

    def gather_rep(buf, sem):
        mine = buf.at[c * 4 + y]
        moves = [(d, push(mine, mine, at_y(d))) for d in (2, 1, 3)]
        push(mine, mine, sibling, recv=sem)
        for d, move in (moves[1], moves[2], moves[0]):
            move.wait_recv()
            got = buf.at[c * 4 + lax.rem(y - d + 4, 4)]
            push(got, got, sibling, recv=sem)
        pltpu.make_async_copy(
            buf.at[pl.ds(0, 4)], buf.at[pl.ds(0, 4)], recv_sem.at[sem]
        ).wait()

    total = reduce_rep(agg_part, y_in2, z_out2, z_in2)
    agg[c * 4 + y] = total
    gather_rep(agg, 91)

    for r in range(4):
        rows = slice(128 * r, 128 * r + 128)
        mine = agg[2 * r : 2 * r + 2].reshape(128, 128)
        pre = dot(left(mine), w_right[...]) + bias[...]
        logistic = 1.0 / (1.0 + jnp.exp(-pre))
        out_stage[rows, :] = pre * logistic
        g = cotangent[rows, :] * logistic * (1.0 + pre * (1.0 - logistic))
        grad[rows, :] = g
        s_right[r] = right(dot(left(g), wt_right[...]))
    out_move = pltpu.make_async_copy(out_stage, out, local_sem.at[4])
    out_move.start()

    chain[16] = jnp.zeros((128, 128), F32)
    chain[33] = jnp.zeros((128, 128), F32)
    for side, table in enumerate((own_table, sib_table)):

        def add_transposed(step, _, side=side, table=table):
            for u in range(4):
                s = step * 4 + u
                row = table[0, 32 + s]
                product = dot(tt_left[16 * side + s], s_right[row])
                chain[17 * side + s] = product + chain[17 * side + table[0, 48 + s]]
            return 0

        lax.fori_loop(0, 4, add_transposed, 0)


    def dense(da, db, j):
        f = chunk(da, db) + j
        return chain[own_table[0, 64 + f]] + chain[17 + sib_table[0, 64 + f]]

    order = (2, -1, 1, 0)
    summed_on_way = (2, -1, 1)
    to_near, to_far = {}, {}
    for k, da in enumerate(order):
        for j in range(2):
            b_far[k, j] = dense(da, 2, j)
            step = 1 - 2 * j if da in summed_on_way else 4 * j - 2
            to_far[k, j] = push(b_far.at[k, j], b_far_in.at[k, j], along_b(step))

    def to_next(k, da):
        for i, d in ((0, 1), (1, -1)):
            b_out[i, k, 1 - i] = dense(da, d, 1 - i)
            b_out[i, k, i] = dense(da, d, i)
            if da in summed_on_way:
                to_far[k, i].wait_recv()
                b_out[i, k, i] += b_far_in[k, i]
            to_near[k, i] = push(b_out.at[i, k], b_in.at[i, k], along_b(d))

    to_next(3, 0)

    gw[...] = dot(left(agg[...].reshape(512, 128).T), right(grad[...]))
    w_out[0:16, :] = gw[pl.ds(pl.multiple_of((c * 4 + y) * 16, 16), 16), :]
    w_out[16:24, :] = jnp.broadcast_to(
        jnp.sum(grad[...], axis=0, keepdims=True), (8, 256)
    )
    x_in5[x] = w_out[...]
    for k, da in enumerate(order[:3]):
        to_next(k, da)
    x_moves = [push(w_out, x_in5.at[x], at_x(d)) for d in (2, 1, 3)]
    for k, da in enumerate(order):
        for j in range(2):
            line[k, j] = dense(da, 0, j)
    for move in x_moves:
        move.wait_recv()
    z_out5[...] = (x_in5[0] + x_in5[1]) + (x_in5[2] + x_in5[3])
    z_in5[zl] = z_out5[...]
    z_moves = [push(z_out5, z_in5.at[zl], at_z(d)) for d in (2, 1, -1)]

    to_a, to_a_far = {}, []
    for k, da in enumerate(order):
        for i in range(2):
            to_near[k, i].wait_recv()
            if da not in summed_on_way:
                to_far[k, i].wait_recv()
        for j in range(2):
            line[k, j] += b_in[0, k, j] + b_in[1, k, j]
            if da not in summed_on_way:
                line[k, j] += b_far_in[k, j]
        if da == 2:
            to_a_far = [
                push(line.at[k, j], a_far_in.at[j], along_a(4 * j - 2)) for j in range(2)
            ]
        elif da != 0:
            i = 0 if da == 1 else 1
            to_a[i] = push(line.at[k], a_in.at[i], along_a(da))
    for move in (*to_a_far, to_a[0], to_a[1]):
        move.wait_recv()
    for j in range(2):
        fin[128 * j : 128 * j + 128, :] = (line[3, j] + a_far_in[j]) + (
            a_in[0, j] + a_in[1, j]
        )
    for move in z_moves:
        move.wait_recv()
    total = reduce_rep(fin, y_in4, z_out4, z_in4)
    here = c * 4 + y
    pay[here, 0:64, :] = total
    summed = (z_in5[0] + z_in5[1]) + (z_in5[2] + z_in5[3])
    pay[here, 64:80, :] = summed[0:16, 0:128]
    pay[here, 80:96, :] = summed[0:16, 128:256]
    grad_bias[...] = summed[16:17, :]
    gather_rep(pay, 92)
    for i in range(8):
        grad_features[64 * i : 64 * i + 64, :] = pay[i, 0:64, :]
        grad_weight[16 * i : 16 * i + 16, 0:128] = pay[i, 64:80, :]
        grad_weight[16 * i : 16 * i + 16, 128:256] = pay[i, 80:96, :]
    out_move.wait()
    for copy in sent:
        copy.wait_send()


def make_table(tile_rows, tile_cols, tile_count):
    lane = lax.broadcasted_iota(jnp.int32, (1, 128), 1)
    slot, part = lax.rem(lane, 16), lax.div(lane, 16)
    spots = []
    for s in range(16):
        col = tile_cols[s]
        spots.append(
            lax.rem(lax.div(col, 2), 2) * 32 + lax.div(col, 4) * 2 + lax.rem(col, 2)
        )
    spot = jnp.zeros((1, 128), jnp.int32)
    row = jnp.zeros((1, 128), jnp.int32)
    for s in range(16):
        spot = jnp.where(slot == s, spots[s], spot)
        row = jnp.where(slot == s, lax.rem(tile_rows[s], 4), row)
    live = slot < tile_count[0]
    spot_here = jnp.where(part >= 4, lane - 64, spot)
    limit = jnp.where(part >= 4, 16, slot)
    found = jnp.full((1, 128), 16, jnp.int32)
    for s in range(16):
        hit = (spot_here == spots[s]) & (limit > s) & (tile_count[0] > s)
        found = jnp.where(hit, s, found)
    table = jnp.where(part == 0, spot, found)
    table = jnp.where(part == 1, jnp.where(live, row, -1), table)
    return jnp.where(part == 2, row, table)


def finish_kernel(*refs):
    sems = refs[8]
    moves = [pltpu.make_async_copy(refs[n], refs[4 + n], sems.at[n]) for n in range(4)]
    for move in moves:
        move.start()
    for move in moves:
        move.wait()


def per_device(features, weight, bias, tile_values, tile_rows, tile_cols, tile_count, cotangent):
    vmem, hbm = pltpu.VMEM, pl.BlockSpec(memory_space=pltpu.HBM)
    smem = pl.BlockSpec(memory_space=pltpu.SMEM)
    anywhere = pl.BlockSpec(memory_space=pl.ANY)
    in_vmem = pl.BlockSpec(memory_space=pltpu.VMEM)
    square = (128, 128)
    shapes = (
        jax.ShapeDtypeStruct((512, 256), F32),
        jax.ShapeDtypeStruct((512, 128), F32),
        jax.ShapeDtypeStruct((128, 256), F32),
        jax.ShapeDtypeStruct((1, 256), F32),
    )
    outs = pl.pallas_call(
        kernel,
        out_shape=shapes,
        in_specs=[smem, smem, smem, hbm, hbm, hbm, hbm, hbm],
        out_specs=(hbm, in_vmem, in_vmem, in_vmem),
        scratch_shapes=[
            vmem((1, 128), jnp.int32),
            vmem((1, 128), jnp.int32),
            pltpu.SMEM((1, 128), jnp.int32),
            pltpu.SMEM((1, 128), jnp.int32),
            vmem((64, *square), F32),
            vmem((32, *square), F32),
            vmem((128, 256), F32),
            vmem((1, 256), F32),
            vmem((512, 256), F32),
            vmem((32, 128, 384), BF16),
            vmem((32, 128, 384), BF16),
            vmem((384, 256), BF16),
            vmem((768, 128), BF16),
            vmem((256, 128), F32),
            vmem((4, 64, 128), F32),
            vmem((64, 128), F32),
            vmem((64, 128), F32),
            vmem((8, 64, 128), F32),
            vmem((512, 256), F32),
            vmem((512, 256), F32),
            vmem((4, 384, 128), BF16),
            vmem((34, *square), F32),
            vmem((2, 4, 2, *square), F32),
            vmem((4, 2, *square), F32),
            vmem((2, 4, 2, *square), F32),
            vmem((4, 2, *square), F32),
            vmem((2, 2, *square), F32),
            vmem((2, *square), F32),
            vmem((4, 2, *square), F32),
            vmem((256, 128), F32),
            vmem((128, 256), F32),
            vmem((24, 256), F32),
            vmem((4, 24, 256), F32),
            vmem((24, 256), F32),
            vmem((4, 24, 256), F32),
            vmem((4, 64, 128), F32),
            vmem((64, 128), F32),
            vmem((64, 128), F32),
            vmem((8, 96, 128), F32),
            pltpu.SemaphoreType.DMA((9,)),
            pltpu.SemaphoreType.DMA((96,)),
            pltpu.SemaphoreType.DMA((96,)),
        ],
        compiler_params=pltpu.CompilerParams(
            collective_id=0, has_side_effects=True, vmem_limit_bytes=60 * 1024 * 1024
        ),
        cost_estimate=pl.CostEstimate(
            flops=400_000_000, bytes_accessed=4_000_000, transcendentals=131072
        ),
    )(
        tile_rows,
        tile_cols,
        tile_count,
        features.reshape(4, *square),
        weight,
        bias[None, :],
        tile_values,
        cotangent,
    )
    output, grad_features, grad_weight, grad_bias = pl.pallas_call(
        finish_kernel,
        out_shape=shapes,
        in_specs=[in_vmem] * 4,
        out_specs=[hbm] * 4,
        scratch_shapes=[pltpu.SemaphoreType.DMA((4,))],
    )(*outs)
    return output, grad_features, grad_weight, grad_bias[0]


def solution(mesh):
    return jax.shard_map(
        per_device,
        mesh=mesh,
        in_specs=(
            P("loop", None),
            P(),
            P(),
            P(("loop", "rep"), None, None),
            P(("loop", "rep")),
            P(("loop", "rep")),
            P(("loop", "rep")),
            P("loop", None),
        ),
        out_specs=(P("loop", None), P("loop", None), P(), P()),
        check_vma=False,
    )
```

time: 92.5 us -> 82 us (0.89)
  local copies, waits for them, and re-layouts: 8.88 us -> 0 us
  Pallas kernels: 81.7 us -> 80.6 us
    unnamed x17 -> x0, local copies, waits for them, and re-layouts: 8.23 us -> none
    pallas_call x1 -> x2, Pallas kernels: 81.7 us -> 80.6 us  [the longest x1 78.5 us: per_device(): pl.pallas_call(kernel, out_shape=shapes, in_specs=[smem, smem, smem, hbm,...]
where the time goes in v2:
time: 82 us; the launch traced here: 81.9 us
  Pallas kernels  80.6 us (98%)
  between operations  1.29 us (2%)
    pallas_call x1, Pallas kernels, per_device(): pl.pallas_call(kernel, out_shape=shapes, in_specs=[smem, smem, smem, hbm,...  78.5 us
    pallas_call x1, Pallas kernels, per_device(): pl.pallas_call(finish_kernel, out_shape=shapes, in_specs=[in_vmem] * 4, o...  2.09 us

profile of v2, /device:TPU:1, one launch (start us, length us, event | category | flops | bytes accessed | tf_op | source)
XLA Modules:
  0.0 81.9 jit_solution(5486108977978778224)
XLA Ops:
  1.3 78.5 %shard_map.111 = (f32[512,256]{1,0:T(8,128)}, f32[512,128]{1,0:T(8,128)}, f32[128,256]{1,0:T(8,128)}, f32[1,256]{1,0:T(1,128)}) custom-call(s32[16]{0:T(128)} %tile_rows.1, s32[16]{0:T(128)} %tile_cols.1, s32[1]{0:T(128)S(6)} %copy.12.tile_count, f32[4,128,128]{2,1,0:T(8,128)} %bitcast.3, f32[128,256]{1,0:T(8,128)} %weight_in.1, f32[1,256]{1,0:T(1,128)} %bitcast.4, ...), custom_call_target="tpu_custom_call" | custom-call | flops 400000000 | bytes 4000000 | tf_op jit(solution)/shard_map/pallas_call | solution.py:417
  79.8 2.1 %shard_map.112 = (f32[512,256]{1,0:T(8,128)}, f32[512,128]{1,0:T(8,128)}, f32[128,256]{1,0:T(8,128)}, f32[1,256]{1,0:T(1,128)}) custom-call(f32[512,256]{1,0:T(8,128)} %get-tuple-element.12.refs_0_, f32[512,128]{1,0:T(8,128)} %get-tuple-element.13.refs_1_, f32[128,256]{1,0:T(8,128)} %get-tuple-element.14.refs_2_, f32[1,256]{1,0:T(1,128)} %get-tuple-element.15.refs_3_), custom_call_target="tpu_custom_call" | custom-call | tf_op jit(solution)/shard_map/pallas_call | solution.py:482

commit v3 on v2

v3 whole, which is shorter than its diff:
```python
import jax
import jax.numpy as jnp
from jax import lax
from jax.experimental import pallas as pl
from jax.experimental.pallas import tpu as pltpu
from jax.sharding import PartitionSpec as P

F32, BF16 = jnp.float32, jnp.bfloat16


def split(v):
    high = v.astype(BF16)
    return high, (v - high.astype(F32)).astype(BF16)


def left(v):
    high, low = split(v)
    return jnp.concatenate([high, high, low], axis=1)


def right(v):
    high, low = split(v)
    return jnp.concatenate([high, low, high], axis=0)


def dot(a, b):
    return lax.dot_general(a, b, (((1,), (0,)), ((), ())), preferred_element_type=F32)


def kernel(
    tile_rows, tile_cols, tile_count, features, weight_in, bias_in, tiles, cotangent_in,
    out, grad_features, grad_weight, grad_bias,
    table_out, table_in, own_table, sib_table, feat, tile, weight, bias, cotangent,
    t_left, tt_left, w_right, wt_right,
    agg_part, core_in, half, y_in2, z_out2, z_in2, agg, out_stage, grad, s_right, chain,
    b_out, b_far, b_in, b_far_in, line, p_in, y_out, y_in4, y_sum, line_in,
    gw, w_out, x_in5, z_out5, z_in5, z_out4, z_in4, pay,
    local_sem, send_sem, recv_sem,
):
    loop, rep = lax.axis_index("loop"), lax.axis_index("rep")
    x, zl = lax.div(loop, 4), lax.rem(loop, 4)
    zh, y, c = lax.div(rep, 8), lax.rem(lax.div(rep, 2), 4), lax.rem(rep, 2)
    z = zh * 4 + zl

    def device(xx, yy, zz, cc):
        return {
            "loop": xx * 4 + lax.rem(zz, 4),
            "rep": lax.div(zz, 4) * 8 + yy * 2 + cc,
        }

    def at_x(d):
        return device(lax.rem(x + d + 4, 4), y, z, c)

    def at_y(d):
        return device(x, lax.rem(y + d + 4, 4), z, c)

    def at_z(d):
        return device(x, y, lax.rem(z + d + 8, 8), c)

    def along_a(d, dy=0):
        return device(
            lax.rem(x + (1 - c) * d + 4, 4),
            lax.rem(y + dy, 4),
            lax.rem(z + c * d + 8, 8),
            c,
        )

    def along_b(d):
        return device(
            lax.rem(x + c * d + 4, 4), y, lax.rem(z + (1 - c) * d + 8, 8), c
        )

    sibling = device(x, y, z, 1 - c)
    a, b = (1 - c) * x + c * zl, c * x + (1 - c) * zl

    def chunk(da, db):
        aa, bb = lax.rem(a + da + 4, 4), lax.rem(b + db + 4, 4)
        return (aa * (4 - 3 * c) + bb * (1 + 3 * c)) * 2

    counter = [0]
    sent = []

    def push(src, dst, to, recv=None):
        n = counter[0]
        counter[0] += 1
        copy = pltpu.make_async_remote_copy(
            src_ref=src,
            dst_ref=dst,
            send_sem=send_sem.at[n],
            recv_sem=recv_sem.at[n if recv is None else recv],
            device_id=to,
            device_id_type=pl.DeviceIdType.MESH,
        )
        copy.start()
        sent.append(copy)
        return copy

    own = pltpu.make_async_copy(
        features.at[pl.ds(4 * c, 4)], feat.at[pl.ds(4 * loop, 4)], local_sem.at[0]
    )
    own.start()
    tiles_in = pltpu.make_async_copy(tiles, tile.at[pl.ds(0, 16)], local_sem.at[2])
    tiles_in.start()
    layer_in = [
        pltpu.make_async_copy(src, dst, local_sem.at[5 + n])
        for n, (src, dst) in enumerate(
            ((weight_in, weight), (bias_in, bias), (cotangent_in, cotangent))
        )
    ]
    for copy in layer_in:
        copy.start()

    partners = [at_x(1), at_x(2), at_x(3), at_y(1), at_y(2), at_y(3)]
    partners += [at_z(1), at_z(2), at_z(6), at_z(7), sibling]
    barrier = pltpu.get_barrier_semaphore()
    for partner in partners:
        pl.semaphore_signal(
            barrier, inc=1, device_id=partner, device_id_type=pl.DeviceIdType.MESH
        )

    table_out[...] = make_table(tile_rows, tile_cols, tile_count)
    table_local = pltpu.make_async_copy(table_out, own_table, local_sem.at[8])
    table_local.start()
    own.wait()
    pl.semaphore_wait(barrier, len(partners))

    def rows_of(da, db, first=0, pieces=4):
        return feat.at[pl.ds(2 * chunk(da, db) + first, pieces)]

    by_pieces = (0,)
    a_near = [push(rows_of(0, 0), rows_of(0, 0), along_a(d)) for d in (1, -1)]
    b_near, b_two, y_spread = {}, {}, []
    two_away = 4 * lax.div(y, 2) - 2

    def far(da, along):
        views = [rows_of(da, 0, 2 * j, 2) for j in range(2)]
        return [push(views[j], views[j], along(4 * j - 2)) for j in range(2)]

    def out_b(da):
        view = rows_of(da, 0, y, 1) if da in by_pieces else rows_of(da, 0)
        b_near[da] = [push(view, view, along_b(d)) for d in (1, -1)]
        if da in by_pieces:
            b_two[da] = [push(view, view, along_b(two_away))]
        elif da == 2:
            b_two[da] = far(da, along_b)

    def near_b(da):
        for i, d in ((0, 1), (1, -1)):
            b_near[da][i].wait_recv()
            if da in by_pieces:
                spread(da, -d)
            elif da != 2:
                view = rows_of(da, -d, 2 * i, 2)
                b_two.setdefault(da, []).append(push(view, view, along_b(d)))
        if da in by_pieces:
            b_two[da][0].wait_recv()
            spread(da, 2)

    def spread(da, db):
        view = rows_of(da, db, y, 1)
        y_spread.extend(push(view, view, at_y(d)) for d in (2, 1, 3))

    out_b(0)
    a_far = far(0, along_a)
    table_move = push(table_out, table_in, sibling)
    tiles_move = push(tiles, tile.at[pl.ds(16, 16)], sibling)

    def split_tiles(start):
        def two(n, _):
            for s in (start + 2 * n, start + 2 * n + 1):
                t_left[s] = left(tile[s])
                tt_left[s] = left(tile[s].T)
            return 0

        lax.fori_loop(0, 8, two, 0)

    near_b(0)
    for i, d in ((0, 1), (1, -1)):
        a_near[i].wait_recv()
        out_b(-d)
    for move in a_far:
        move.wait_recv()
    out_b(2)
    table_local.wait()
    table_move.wait_recv()
    table_local = pltpu.make_async_copy(table_in, sib_table, local_sem.at[3])
    table_local.start()
    tiles_in.wait()
    split_tiles(0)
    near_b(-1)
    near_b(1)
    tiles_move.wait_recv()
    split_tiles(16)
    for copy in layer_in:
        copy.wait()
    chain[16] = jnp.zeros((128, 128), F32)
    chain[33] = jnp.zeros((128, 128), F32)
    w_right[...] = right(weight[...])
    wt_right[...] = right(weight[...].T)
    table_local.wait()
    near_b(2)
    for da in (-1, 1, 2):
        if da not in by_pieces:
            for move in b_two[da]:
                move.wait_recv()
    for move in y_spread:
        move.wait_recv()

    for side, table in enumerate((own_table, sib_table)):

        def add_products(step, _, side=side, table=table):
            for u in range(4):
                s = step * 4 + u
                spot = 2 * lax.rem(table[0, s], 32)
                block = right(feat[pl.ds(spot, 2)].reshape(128, 128))
                product = dot(t_left[16 * side + s], block)
                chain[17 * side + s] = product + chain[17 * side + table[0, 16 + s]]
            return 0

        lax.fori_loop(0, 4, add_products, 0)
    for j in range(4):
        f = 4 * c + j
        agg_part[j] = chain[own_table[1, f]] + chain[17 + sib_table[1, f]]

    other = push(agg_part.at[pl.ds(2 * (1 - c), 2)], core_in, sibling)
    other.wait_recv()
    for j in range(2):
        half[128 * j : 128 * j + 128, :] = agg_part[2 * c + j] + core_in[j]

    def sum_z(value, z_out, z_in):
        z_out[...] = value
        swap = push(z_out, z_in, at_z(4))
        swap.wait_recv()
        return z_out[...] + z_in[...]

    def reduce_rep(part, y_in, z_out, z_in):
        moves = []
        for d in (2, 1, 3):
            there = lax.rem(y + d, 4)
            moves.append(
                push(part.at[pl.ds(there * 64, 64)], y_in.at[y], at_y(d))
            )
        y_in[y] = part[pl.ds(pl.multiple_of(y * 64, 64), 64), :]
        for move in moves:
            move.wait_recv()
        return sum_z((y_in[0] + y_in[1]) + (y_in[2] + y_in[3]), z_out, z_in)

    def gather_rep(buf, sem):
        mine = buf.at[c * 4 + y]
        moves = [(d, push(mine, mine, at_y(d))) for d in (2, 1, 3)]
        push(mine, mine, sibling, recv=sem)
        for d, move in (moves[1], moves[2], moves[0]):
            move.wait_recv()
            got = buf.at[c * 4 + lax.rem(y - d + 4, 4)]
            push(got, got, sibling, recv=sem)
        pltpu.make_async_copy(
            buf.at[pl.ds(0, 4)], buf.at[pl.ds(0, 4)], recv_sem.at[sem]
        ).wait()

    total = reduce_rep(half, y_in2, z_out2, z_in2)
    agg[c * 4 + y] = total
    gather_rep(agg, 111)

    for r in range(4):
        rows = slice(128 * r, 128 * r + 128)
        mine = agg[2 * r : 2 * r + 2].reshape(128, 128)
        pre = dot(left(mine), w_right[...]) + bias[...]
        logistic = 1.0 / (1.0 + jnp.exp(-pre))
        out_stage[rows, :] = pre * logistic
        g = cotangent[rows, :] * logistic * (1.0 + pre * (1.0 - logistic))
        grad[rows, :] = g
        s_right[r] = right(dot(left(g), wt_right[...]))
    out_move = pltpu.make_async_copy(out_stage, out, local_sem.at[4])
    out_move.start()

    for side, table in enumerate((own_table, sib_table)):

        def add_transposed(step, _, side=side, table=table):
            for u in range(4):
                s = step * 4 + u
                row = table[0, 32 + s]
                product = dot(tt_left[16 * side + s], s_right[row])
                chain[17 * side + s] = product + chain[17 * side + table[0, 48 + s]]
            return 0

        lax.fori_loop(0, 4, add_transposed, 0)


    def dense(da, db, j):
        f = 64 + 32 * c + chunk(da, db) + j
        return chain[own_table[0, f]] + chain[17 + sib_table[0, f]]

    order = (2, -1, 1, 0)
    to_near, to_far = {}, {}
    for k, da in enumerate(order[:3]):
        for j in range(2):
            b_far[k, j] = dense(da, 2, j)
            to_far[k, j] = push(b_far.at[k, j], b_far_in.at[k, j], along_b(1 - 2 * j))

    y_moves = []
    for n, db in enumerate((2, -1, 1, 0)):
        for j in range(2):
            y_out[n, 2 * j : 2 * j + 2] = dense(0, db, j).reshape(2, 64, 128)
        for dy in (2, 1, 3):
            piece = lax.rem(y + dy, 4)
            y_moves.append(push(y_out.at[n, piece], y_in4.at[n, dy - 1], at_y(dy)))

    def to_next(k, da):
        for i, d in ((0, 1), (1, -1)):
            b_out[i, k, 1 - i] = dense(da, d, 1 - i)
            to_far[k, i].wait_recv()
            b_out[i, k, i] = dense(da, d, i) + b_far_in[k, i]
            to_near[k, i] = push(b_out.at[i, k], b_in.at[i, k], along_b(d))

    gw[...] = dot(left(agg[...].reshape(512, 128).T), right(grad[...]))
    w_out[0:16, :] = gw[pl.ds(pl.multiple_of((c * 4 + y) * 16, 16), 16), :]
    w_out[16:24, :] = jnp.broadcast_to(
        jnp.sum(grad[...], axis=0, keepdims=True), (8, 256)
    )
    x_in5[x] = w_out[...]
    x_moves = [push(w_out, x_in5.at[x], at_x(d)) for d in (2, 1, 3)]
    for k, da in enumerate(order[:3]):
        to_next(k, da)
    for move in y_moves:
        move.wait_recv()
    line_moves = []
    for n, d in enumerate((two_away, -1, 1, 0)):
        y_sum[n] = (y_out[n, y] + y_in4[n, 0]) + (y_in4[n, 1] + y_in4[n, 2])
        if n < 3:
            line_moves.append(push(y_sum.at[n], line_in.at[n], along_b(d)))

    pieces = []
    for k, da in enumerate(order[:3]):
        for i in range(2):
            to_near[k, i].wait_recv()
        for j in range(2):
            value = dense(da, 0, j) + (b_in[0, k, j] + b_in[1, k, j])
            line[k, 2 * j : 2 * j + 2] = value.reshape(2, 64, 128)
        for dy in (2, 1, 3, 0):
            piece = lax.rem(y + dy, 4)
            d = 4 * lax.div(piece, 2) - 2 if da == 2 else da
            pieces.append(push(line.at[k, piece], p_in.at[k, dy], along_a(d, dy)))
    for move in x_moves:
        move.wait_recv()
    z_out5[...] = (x_in5[0] + x_in5[1]) + (x_in5[2] + x_in5[3])
    z_in5[zl] = z_out5[...]
    z_moves = [push(z_out5, z_in5.at[zl], at_z(d)) for d in (2, 1, -1)]
    total = y_sum[3]
    for n in range(3):
        line_moves[n].wait_recv()
        total += line_in[n]
    for k in range(3):
        for n, dy in enumerate((2, 1, 3, 0)):
            pieces[4 * k + n].wait_recv()
            total += p_in[k, dy]
    total = sum_z(total, z_out4, z_in4)
    for move in z_moves:
        move.wait_recv()
    here = c * 4 + y
    pay[here, 0:64, :] = total
    summed = (z_in5[0] + z_in5[1]) + (z_in5[2] + z_in5[3])
    pay[here, 64:80, :] = summed[0:16, 0:128]
    pay[here, 80:96, :] = summed[0:16, 128:256]
    grad_bias[...] = summed[16:17, :]
    gather_rep(pay, 112)
    for i in range(8):
        grad_features[64 * i : 64 * i + 64, :] = pay[i, 0:64, :]
        grad_weight[16 * i : 16 * i + 16, 0:128] = pay[i, 64:80, :]
        grad_weight[16 * i : 16 * i + 16, 128:256] = pay[i, 80:96, :]
    out_move.wait()
    for copy in sent:
        copy.wait_send()


def make_table(tile_rows, tile_cols, tile_count):
    lane = lax.broadcasted_iota(jnp.int32, (1, 128), 1)
    slot, part = lax.rem(lane, 16), lax.div(lane, 16)
    spots, lines = [], []
    for s in range(16):
        col = tile_cols[s]
        side = lax.rem(lax.div(col, 2), 2)
        spots.append(side * 32 + lax.div(col, 4) * 2 + lax.rem(col, 2))
        lines.append(side * 4 + lax.rem(tile_rows[s], 4))
    spot = jnp.zeros((1, 128), jnp.int32)
    line = jnp.zeros((1, 128), jnp.int32)
    for s in range(16):
        spot = jnp.where(slot == s, spots[s], spot)
        line = jnp.where(slot == s, lines[s], line)
    by_spot = jnp.where(part >= 4, lane - 64, spot)
    limit = jnp.where(part >= 4, 16, slot)
    found = jnp.full((1, 128), 16, jnp.int32)
    found_line, last_line = found, found
    for s in range(16):
        live = tile_count[0] > s
        found = jnp.where((by_spot == spots[s]) & (limit > s) & live, s, found)
        found_line = jnp.where((line == lines[s]) & (slot > s) & live, s, found_line)
        last_line = jnp.where((lane == lines[s]) & live, s, last_line)
    table = jnp.where(part == 0, spot, found)
    table = jnp.where(part == 1, found_line, table)
    table = jnp.where(part == 2, lax.rem(line, 4), table)
    return jnp.concatenate([table, last_line], axis=0)


def finish_kernel(*refs):
    sems = refs[8]
    moves = [pltpu.make_async_copy(refs[n], refs[4 + n], sems.at[n]) for n in range(4)]
    for move in moves:
        move.start()
    for move in moves:
        move.wait()


def per_device(features, weight, bias, tile_values, tile_rows, tile_cols, tile_count, cotangent):
    vmem, hbm = pltpu.VMEM, pl.BlockSpec(memory_space=pltpu.HBM)
    smem = pl.BlockSpec(memory_space=pltpu.SMEM)
    anywhere = pl.BlockSpec(memory_space=pl.ANY)
    in_vmem = pl.BlockSpec(memory_space=pltpu.VMEM)
    square = (128, 128)
    shapes = (
        jax.ShapeDtypeStruct((512, 256), F32),
        jax.ShapeDtypeStruct((512, 128), F32),
        jax.ShapeDtypeStruct((128, 256), F32),
        jax.ShapeDtypeStruct((1, 256), F32),
    )
    outs = pl.pallas_call(
        kernel,
        out_shape=shapes,
        in_specs=[smem, smem, smem, hbm, hbm, hbm, hbm, hbm],
        out_specs=(hbm, in_vmem, in_vmem, in_vmem),
        scratch_shapes=[
            vmem((2, 128), jnp.int32),
            vmem((2, 128), jnp.int32),
            pltpu.SMEM((2, 128), jnp.int32),
            pltpu.SMEM((2, 128), jnp.int32),
            vmem((64, 64, 128), F32),
            vmem((32, *square), F32),
            vmem((128, 256), F32),
            vmem((1, 256), F32),
            vmem((512, 256), F32),
            vmem((32, 128, 384), BF16),
            vmem((32, 128, 384), BF16),
            vmem((384, 256), BF16),
            vmem((768, 128), BF16),
            vmem((4, *square), F32),
            vmem((2, *square), F32),
            vmem((256, 128), F32),
            vmem((4, 64, 128), F32),
            vmem((64, 128), F32),
            vmem((64, 128), F32),
            vmem((8, 64, 128), F32),
            vmem((512, 256), F32),
            vmem((512, 256), F32),
            vmem((4, 384, 128), BF16),
            vmem((34, *square), F32),
            vmem((2, 4, 2, *square), F32),
            vmem((4, 2, *square), F32),
            vmem((2, 4, 2, *square), F32),
            vmem((4, 2, *square), F32),
            vmem((3, 4, 64, 128), F32),
            vmem((3, 4, 64, 128), F32),
            vmem((4, 4, 64, 128), F32),
            vmem((4, 3, 64, 128), F32),
            vmem((4, 64, 128), F32),
            vmem((3, 64, 128), F32),
            vmem((128, 256), F32),
            vmem((24, 256), F32),
            vmem((4, 24, 256), F32),
            vmem((24, 256), F32),
            vmem((4, 24, 256), F32),
            vmem((64, 128), F32),
            vmem((64, 128), F32),
            vmem((8, 96, 128), F32),
            pltpu.SemaphoreType.DMA((9,)),
            pltpu.SemaphoreType.DMA((120,)),
            pltpu.SemaphoreType.DMA((120,)),
        ],
        compiler_params=pltpu.CompilerParams(
            collective_id=0, has_side_effects=True, vmem_limit_bytes=60 * 1024 * 1024
        ),
        cost_estimate=pl.CostEstimate(
            flops=400_000_000, bytes_accessed=4_000_000, transcendentals=131072
        ),
    )(
        tile_rows,
        tile_cols,
        tile_count,
        features.reshape(8, 64, 128),
        weight,
        bias[None, :],
        tile_values,
        cotangent,
    )
    output, grad_features, grad_weight, grad_bias = pl.pallas_call(
        finish_kernel,
        out_shape=shapes,
        in_specs=[in_vmem] * 4,
        out_specs=[hbm] * 4,
        scratch_shapes=[pltpu.SemaphoreType.DMA((4,))],
    )(*outs)
    return output, grad_features, grad_weight, grad_bias[0]


def solution(mesh):
    return jax.shard_map(
        per_device,
        mesh=mesh,
        in_specs=(
            P("loop", None),
            P(),
            P(),
            P(("loop", "rep"), None, None),
            P(("loop", "rep")),
            P(("loop", "rep")),
            P(("loop", "rep")),
            P("loop", None),
        ),
        out_specs=(P("loop", None), P("loop", None), P(), P()),
        check_vma=False,
    )
```

time: 82 us -> 77.9 us (0.950)
  Pallas kernels: 80.6 us -> 76.5 us
    pallas_call x1, Pallas kernels: 78.5 us -> 74.4 us  [per_device(): pl.pallas_call(kernel, out_shape=shapes, in_specs=[smem, smem, smem, hbm,...]
where the time goes in v3:
time: 77.9 us; the launch traced here: 77.8 us
  Pallas kernels  76.5 us (98%)
  between operations  1.29 us (2%)
    pallas_call x1, Pallas kernels, per_device(): pl.pallas_call(kernel, out_shape=shapes, in_specs=[smem, smem, smem, hbm,...  74.4 us
    pallas_call x1, Pallas kernels, per_device(): pl.pallas_call(finish_kernel, out_shape=shapes, in_specs=[in_vmem] * 4, o...  2.09 us

profile of v3, /device:TPU:1, one launch (start us, length us, event | category | flops | bytes accessed | tf_op | source)
XLA Modules:
  0.0 77.8 jit_solution(10976999325436330015)
XLA Ops:
  1.3 74.4 %shard_map.111 = (f32[512,256]{1,0:T(8,128)}, f32[512,128]{1,0:T(8,128)}, f32[128,256]{1,0:T(8,128)}, f32[1,256]{1,0:T(1,128)}) custom-call(s32[16]{0:T(128)} %tile_rows.1, s32[16]{0:T(128)} %tile_cols.1, s32[1]{0:T(128)S(6)} %copy.12.tile_count, f32[8,64,128]{2,1,0:T(8,128)} %bitcast.3, f32[128,256]{1,0:T(8,128)} %weight_in.1, f32[1,256]{1,0:T(1,128)} %bitcast.4, ...), custom_call_target="tpu_custom_call" | custom-call | flops 400000000 | bytes 4000000 | tf_op jit(solution)/shard_map/pallas_call | solution.py:425
  75.7 2.1 %shard_map.112 = (f32[512,256]{1,0:T(8,128)}, f32[512,128]{1,0:T(8,128)}, f32[128,256]{1,0:T(8,128)}, f32[1,256]{1,0:T(1,128)}) custom-call(f32[512,256]{1,0:T(8,128)} %get-tuple-element.12.refs_0_, f32[512,128]{1,0:T(8,128)} %get-tuple-element.13.refs_1_, f32[128,256]{1,0:T(8,128)} %get-tuple-element.14.refs_2_, f32[1,256]{1,0:T(1,128)} %get-tuple-element.15.refs_3_), custom_call_target="tpu_custom_call" | custom-call | tf_op jit(solution)/shard_map/pallas_call | solution.py:493

commit v4 on v3

--- a/solution.py
+++ b/solution.py
@@ -28,9 +28,9 @@
 
 
 def kernel(
-    tile_rows, tile_cols, tile_count, features, weight_in, bias_in, tiles, cotangent_in,
+    rows_in, cols_in, count_in, features, weight_in, bias_in, tiles, cotangent_in,
     out, grad_features, grad_weight, grad_bias,
-    table_out, table_in, own_table, sib_table, feat, tile, weight, bias, cotangent,
+    tile_rows, tile_cols, tile_count, table_out, table_in, own_table, sib_table, feat, tile, weight, bias, cotangent,
     t_left, tt_left, w_right, wt_right,
     agg_part, core_in, half, y_in2, z_out2, z_in2, agg, out_stage, grad, s_right, chain,
     b_out, b_far, b_in, b_far_in, line, p_in, y_out, y_in4, y_sum, line_in,
@@ -95,10 +95,26 @@
         sent.append(copy)
         return copy
 
+    partners = [at_x(1), at_x(2), at_x(3), at_y(1), at_y(2), at_y(3)]
+    partners += [at_z(1), at_z(2), at_z(6), at_z(7), sibling]
+    barrier = pltpu.get_barrier_semaphore()
+    for partner in partners:
+        pl.semaphore_signal(
+            barrier, inc=1, device_id=partner, device_id_type=pl.DeviceIdType.MESH
+        )
+
     own = pltpu.make_async_copy(
         features.at[pl.ds(4 * c, 4)], feat.at[pl.ds(4 * loop, 4)], local_sem.at[0]
     )
     own.start()
+    slots_in = [
+        pltpu.make_async_copy(src, dst, local_sem.at[9 + n])
+        for n, (src, dst) in enumerate(
+            ((rows_in, tile_rows), (cols_in, tile_cols), (count_in, tile_count))
+        )
+    ]
+    for copy in slots_in:
+        copy.start()
     tiles_in = pltpu.make_async_copy(tiles, tile.at[pl.ds(0, 16)], local_sem.at[2])
     tiles_in.start()
     layer_in = [
@@ -110,14 +126,8 @@
     for copy in layer_in:
         copy.start()
 
-    partners = [at_x(1), at_x(2), at_x(3), at_y(1), at_y(2), at_y(3)]
-    partners += [at_z(1), at_z(2), at_z(6), at_z(7), sibling]
-    barrier = pltpu.get_barrier_semaphore()
-    for partner in partners:
-        pl.semaphore_signal(
-            barrier, inc=1, device_id=partner, device_id_type=pl.DeviceIdType.MESH
-        )
-
+    for copy in slots_in:
+        copy.wait()
     table_out[...] = make_table(tile_rows, tile_cols, tile_count)
     table_local = pltpu.make_async_copy(table_out, own_table, local_sem.at[8])
     table_local.start()
@@ -206,18 +216,13 @@
     for move in y_spread:
         move.wait_recv()
 
-    for side, table in enumerate((own_table, sib_table)):
-
-        def add_products(step, _, side=side, table=table):
-            for u in range(4):
-                s = step * 4 + u
-                spot = 2 * lax.rem(table[0, s], 32)
-                block = right(feat[pl.ds(spot, 2)].reshape(128, 128))
-                product = dot(t_left[16 * side + s], block)
-                chain[17 * side + s] = product + chain[17 * side + table[0, 16 + s]]
-            return 0
-
-        lax.fori_loop(0, 4, add_products, 0)
+    tables = (own_table, sib_table)
+    for s in range(16):
+        for side, table in enumerate(tables):
+            spot = 2 * lax.rem(table[0, s], 32)
+            block = right(feat[pl.ds(spot, 2)].reshape(128, 128))
+            product = dot(t_left[16 * side + s], block)
+            chain[17 * side + s] = product + chain[17 * side + table[0, 16 + s]]
     for j in range(4):
         f = 4 * c + j
         agg_part[j] = chain[own_table[1, f]] + chain[17 + sib_table[1, f]]
@@ -249,7 +254,7 @@
         mine = buf.at[c * 4 + y]
         moves = [(d, push(mine, mine, at_y(d))) for d in (2, 1, 3)]
         push(mine, mine, sibling, recv=sem)
-        for d, move in (moves[1], moves[2], moves[0]):
+        for d, move in moves[1:] + moves[:1]:
             move.wait_recv()
             got = buf.at[c * 4 + lax.rem(y - d + 4, 4)]
             push(got, got, sibling, recv=sem)
@@ -273,18 +278,10 @@
     out_move = pltpu.make_async_copy(out_stage, out, local_sem.at[4])
     out_move.start()
 
-    for side, table in enumerate((own_table, sib_table)):
-
-        def add_transposed(step, _, side=side, table=table):
-            for u in range(4):
-                s = step * 4 + u
-                row = table[0, 32 + s]
-                product = dot(tt_left[16 * side + s], s_right[row])
-                chain[17 * side + s] = product + chain[17 * side + table[0, 48 + s]]
-            return 0
-
-        lax.fori_loop(0, 4, add_transposed, 0)
-
+    for s in range(16):
+        for side, table in enumerate(tables):
+            product = dot(tt_left[16 * side + s], s_right[table[0, 32 + s]])
+            chain[17 * side + s] = product + chain[17 * side + table[0, 48 + s]]
 
     def dense(da, db, j):
         f = 64 + 32 * c + chunk(da, db) + j
@@ -412,8 +409,6 @@
 
 def per_device(features, weight, bias, tile_values, tile_rows, tile_cols, tile_count, cotangent):
     vmem, hbm = pltpu.VMEM, pl.BlockSpec(memory_space=pltpu.HBM)
-    smem = pl.BlockSpec(memory_space=pltpu.SMEM)
-    anywhere = pl.BlockSpec(memory_space=pl.ANY)
     in_vmem = pl.BlockSpec(memory_space=pltpu.VMEM)
     square = (128, 128)
     shapes = (
@@ -425,9 +420,12 @@
     outs = pl.pallas_call(
         kernel,
         out_shape=shapes,
-        in_specs=[smem, smem, smem, hbm, hbm, hbm, hbm, hbm],
+        in_specs=[hbm] * 8,
         out_specs=(hbm, in_vmem, in_vmem, in_vmem),
         scratch_shapes=[
+            pltpu.SMEM((16,), jnp.int32),
+            pltpu.SMEM((16,), jnp.int32),
+            pltpu.SMEM((1,), jnp.int32),
             vmem((2, 128), jnp.int32),
             vmem((2, 128), jnp.int32),
             pltpu.SMEM((2, 128), jnp.int32),
@@ -470,7 +468,7 @@
             vmem((64, 128), F32),
             vmem((64, 128), F32),
             vmem((8, 96, 128), F32),
-            pltpu.SemaphoreType.DMA((9,)),
+            pltpu.SemaphoreType.DMA((12,)),
             pltpu.SemaphoreType.DMA((120,)),
             pltpu.SemaphoreType.DMA((120,)),
         ],

time: 77.9 us -> 75.1 us (0.964)
  Pallas kernels: 76.5 us -> 73.7 us
    pallas_call x1, Pallas kernels: 74.4 us -> 71.6 us  [per_device(): pl.pallas_call(kernel, out_shape=shapes, in_specs=[hbm] * 8, out_specs=(h...]
where the time goes in v4:
time: 75.1 us; the launch traced here: 75 us
  Pallas kernels  73.7 us (98%)
  between operations  1.29 us (2%)
    pallas_call x1, Pallas kernels, per_device(): pl.pallas_call(kernel, out_shape=shapes, in_specs=[hbm] * 8, out_specs=(h...  71.6 us
    pallas_call x1, Pallas kernels, per_device(): pl.pallas_call(finish_kernel, out_shape=shapes, in_specs=[in_vmem] * 4, o...  2.09 us

profile of v4, /device:TPU:1, one launch (start us, length us, event | category | flops | bytes accessed | tf_op | source)
XLA Modules:
  0.0 75.0 jit_solution(6273423566681018490)
XLA Ops:
  1.3 71.6 %shard_map.111 = (f32[512,256]{1,0:T(8,128)}, f32[512,128]{1,0:T(8,128)}, f32[128,256]{1,0:T(8,128)}, f32[1,256]{1,0:T(1,128)}) custom-call(s32[16]{0:T(128)} %rows_in.1, s32[16]{0:T(128)} %cols_in.1, s32[1]{0:T(128)S(6)} %copy.12.count_in, f32[8,64,128]{2,1,0:T(8,128)} %bitcast.3, f32[128,256]{1,0:T(8,128)} %weight_in.1, f32[1,256]{1,0:T(1,128)} %bitcast.4, ...), custom_call_target="tpu_custom_call" | custom-call | flops 400000000 | bytes 4000000 | tf_op jit(solution)/shard_map/pallas_call | solution.py:420
  72.9 2.1 %shard_map.112 = (f32[512,256]{1,0:T(8,128)}, f32[512,128]{1,0:T(8,128)}, f32[128,256]{1,0:T(8,128)}, f32[1,256]{1,0:T(1,128)}) custom-call(f32[512,256]{1,0:T(8,128)} %get-tuple-element.12.refs_0_, f32[512,128]{1,0:T(8,128)} %get-tuple-element.13.refs_1_, f32[128,256]{1,0:T(8,128)} %get-tuple-element.14.refs_2_, f32[1,256]{1,0:T(1,128)} %get-tuple-element.15.refs_3_), custom_call_target="tpu_custom_call" | custom-call | tf_op jit(solution)/shard_map/pallas_call | solution.py:491

commit v5 on v4

--- a/solution.py
+++ b/solution.py
@@ -234,7 +234,11 @@
 
     def sum_z(value, z_out, z_in):
         z_out[...] = value
+        earlier = len(sent)
         swap = push(z_out, z_in, at_z(4))
+        for copy in sent[:earlier]:
+            copy.wait_send()
+        del sent[:earlier]
         swap.wait_recv()
         return z_out[...] + z_in[...]
 
@@ -258,23 +262,29 @@
             move.wait_recv()
             got = buf.at[c * 4 + lax.rem(y - d + 4, 4)]
             push(got, got, sibling, recv=sem)
-        pltpu.make_async_copy(
+        return pltpu.make_async_copy(
             buf.at[pl.ds(0, 4)], buf.at[pl.ds(0, 4)], recv_sem.at[sem]
-        ).wait()
+        )
 
     total = reduce_rep(half, y_in2, z_out2, z_in2)
     agg[c * 4 + y] = total
-    gather_rep(agg, 111)
-
-    for r in range(4):
-        rows = slice(128 * r, 128 * r + 128)
-        mine = agg[2 * r : 2 * r + 2].reshape(128, 128)
+    others = gather_rep(agg, 111)
+
+    def layer(r):
+        rows = pl.ds(pl.multiple_of(128 * r, 128), 128)
+        mine = agg[pl.ds(2 * r, 2)].reshape(128, 128)
         pre = dot(left(mine), w_right[...]) + bias[...]
         logistic = 1.0 / (1.0 + jnp.exp(-pre))
         out_stage[rows, :] = pre * logistic
         g = cotangent[rows, :] * logistic * (1.0 + pre * (1.0 - logistic))
         grad[rows, :] = g
         s_right[r] = right(dot(left(g), wt_right[...]))
+
+    layer(2 * c)
+    layer(2 * c + 1)
+    others.wait()
+    layer(2 - 2 * c)
+    layer(3 - 2 * c)
     out_move = pltpu.make_async_copy(out_stage, out, local_sem.at[4])
     out_move.start()
 
@@ -359,7 +369,7 @@
     pay[here, 64:80, :] = summed[0:16, 0:128]
     pay[here, 80:96, :] = summed[0:16, 128:256]
     grad_bias[...] = summed[16:17, :]
-    gather_rep(pay, 112)
+    gather_rep(pay, 112).wait()
     for i in range(8):
         grad_features[64 * i : 64 * i + 64, :] = pay[i, 0:64, :]
         grad_weight[16 * i : 16 * i + 16, 0:128] = pay[i, 64:80, :]
@@ -399,12 +409,21 @@
 
 
 def finish_kernel(*refs):
-    sems = refs[8]
-    moves = [pltpu.make_async_copy(refs[n], refs[4 + n], sems.at[n]) for n in range(4)]
-    for move in moves:
-        move.start()
-    for move in moves:
-        move.wait()
+    sources, results, through, sems = refs[:4], refs[4:8], refs[8:12], refs[12]
+    moves = [
+        (
+            pltpu.make_async_copy(sources[n], through[n], sems.at[n]),
+            pltpu.make_async_copy(through[n], results[n], sems.at[n]),
+        )
+        for n in range(4)
+    ]
+    for read, _ in moves:
+        read.start()
+    for read, write in moves:
+        read.wait()
+        write.start()
+    for _, write in moves:
+        write.wait()
 
 
 def per_device(features, weight, bias, tile_values, tile_rows, tile_cols, tile_count, cotangent):
@@ -469,8 +488,8 @@
             vmem((64, 128), F32),
             vmem((8, 96, 128), F32),
             pltpu.SemaphoreType.DMA((12,)),
-            pltpu.SemaphoreType.DMA((120,)),
-            pltpu.SemaphoreType.DMA((120,)),
+            pltpu.SemaphoreType.DMA((113,)),
+            pltpu.SemaphoreType.DMA((113,)),
         ],
         compiler_params=pltpu.CompilerParams(
             collective_id=0, has_side_effects=True, vmem_limit_bytes=60 * 1024 * 1024
@@ -491,9 +510,10 @@
     output, grad_features, grad_weight, grad_bias = pl.pallas_call(
         finish_kernel,
         out_shape=shapes,
-        in_specs=[in_vmem] * 4,
+        in_specs=[hbm] * 4,
         out_specs=[hbm] * 4,
-        scratch_shapes=[pltpu.SemaphoreType.DMA((4,))],
+        scratch_shapes=[vmem(v.shape, F32) for v in shapes]
+        + [pltpu.SemaphoreType.DMA((4,))],
     )(*outs)
     return output, grad_features, grad_weight, grad_bias[0]
 

time: 75.1 us -> 74.8 us (level)
  no operation moved by 1% of the time
where the time goes in v5:
time: 74.8 us; the launch traced here: 74.7 us
  Pallas kernels  73.4 us (98%)
  between operations  1.29 us (2%)
    pallas_call x1, Pallas kernels, per_device(): pl.pallas_call(kernel, out_shape=shapes, in_specs=[hbm] * 8, out_specs=(h...  71.4 us
    pallas_call x1, Pallas kernels, per_device(): pl.pallas_call(finish_kernel, out_shape=shapes, in_specs=[hbm] * 4, out_s...  1.99 us

profile of v5, /device:TPU:1, one launch (start us, length us, event | category | flops | bytes accessed | tf_op | source)
XLA Modules:
  0.0 74.7 jit_solution(17170949595971134992)
XLA Ops:
  1.3 71.4 %shard_map.111 = (f32[512,256]{1,0:T(8,128)}, f32[512,128]{1,0:T(8,128)}, f32[128,256]{1,0:T(8,128)}, f32[1,256]{1,0:T(1,128)}) custom-call(s32[16]{0:T(128)} %rows_in.1, s32[16]{0:T(128)} %cols_in.1, s32[1]{0:T(128)S(6)} %copy.12.count_in, f32[8,64,128]{2,1,0:T(8,128)} %bitcast.3, f32[128,256]{1,0:T(8,128)} %weight_in.1, f32[1,256]{1,0:T(1,128)} %bitcast.4, ...), custom_call_target="tpu_custom_call" | custom-call | flops 400000000 | bytes 4000000 | tf_op jit(solution)/shard_map/pallas_call | solution.py:439
  72.7 2.0 %shard_map.112 = (f32[512,256]{1,0:T(8,128)}, f32[512,128]{1,0:T(8,128)}, f32[128,256]{1,0:T(8,128)}, f32[1,256]{1,0:T(1,128)}) custom-call(f32[512,256]{1,0:T(8,128)} %get-tuple-element.12.refs_0_, f32[512,128]{1,0:T(8,128)} %get-tuple-element.13.refs_1_, f32[128,256]{1,0:T(8,128)} %get-tuple-element.14.refs_2_, f32[1,256]{1,0:T(1,128)} %get-tuple-element.15.refs_3_), custom_call_target="tpu_custom_call" | custom-call | tf_op jit(solution)/shard_map/pallas_call | solution.py:510

commit v6 on v5

--- a/solution.py
+++ b/solution.py
@@ -34,7 +34,7 @@
     t_left, tt_left, w_right, wt_right,
     agg_part, core_in, half, y_in2, z_out2, z_in2, agg, out_stage, grad, s_right, chain,
     b_out, b_far, b_in, b_far_in, line, p_in, y_out, y_in4, y_sum, line_in,
-    gw, w_out, x_in5, z_out5, z_in5, z_out4, z_in4, pay,
+    gw, w_out, x_in5, z_out5, z_in5, z_out4, z_in4, pay, pay_w,
     local_sem, send_sem, recv_sem,
 ):
     loop, rep = lax.axis_index("loop"), lax.axis_index("rep")
@@ -232,14 +232,17 @@
     for j in range(2):
         half[128 * j : 128 * j + 128, :] = agg_part[2 * c + j] + core_in[j]
 
-    def sum_z(value, z_out, z_in):
+    def sum_z(value, z_out, z_in, meanwhile=None):
         z_out[...] = value
         earlier = len(sent)
         swap = push(z_out, z_in, at_z(4))
         for copy in sent[:earlier]:
             copy.wait_send()
         del sent[:earlier]
+        begun = meanwhile() if meanwhile else None
         swap.wait_recv()
+        if meanwhile:
+            return z_out[...] + z_in[...], begun
         return z_out[...] + z_in[...]
 
     def reduce_rep(part, y_in, z_out, z_in):
@@ -254,10 +257,15 @@
             move.wait_recv()
         return sum_z((y_in[0] + y_in[1]) + (y_in[2] + y_in[3]), z_out, z_in)
 
-    def gather_rep(buf, sem):
+    def gather_start(buf, sem):
         mine = buf.at[c * 4 + y]
         moves = [(d, push(mine, mine, at_y(d))) for d in (2, 1, 3)]
         push(mine, mine, sibling, recv=sem)
+        return moves
+
+    def gather_rep(buf, sem, moves=None):
+        if moves is None:
+            moves = gather_start(buf, sem)
         for d, move in moves[1:] + moves[:1]:
             move.wait_recv()
             got = buf.at[c * 4 + lax.rem(y - d + 4, 4)]
@@ -360,20 +368,28 @@
         for n, dy in enumerate((2, 1, 3, 0)):
             pieces[4 * k + n].wait_recv()
             total += p_in[k, dy]
-    total = sum_z(total, z_out4, z_in4)
-    for move in z_moves:
-        move.wait_recv()
     here = c * 4 + y
-    pay[here, 0:64, :] = total
-    summed = (z_in5[0] + z_in5[1]) + (z_in5[2] + z_in5[3])
-    pay[here, 64:80, :] = summed[0:16, 0:128]
-    pay[here, 80:96, :] = summed[0:16, 128:256]
-    grad_bias[...] = summed[16:17, :]
-    gather_rep(pay, 112).wait()
+
+    def weight_part():
+        for move in z_moves:
+            move.wait_recv()
+        summed = (z_in5[0] + z_in5[1]) + (z_in5[2] + z_in5[3])
+        pay_w[here, 0:16, :] = summed[0:16, 0:128]
+        pay_w[here, 16:32, :] = summed[0:16, 128:256]
+        grad_bias[...] = summed[16:17, :]
+        return gather_start(pay_w, 110)
+
+    total, begun = sum_z(total, z_out4, z_in4, weight_part)
+    pay[here] = total
+    moves = gather_start(pay, 112)
+    weight_others = gather_rep(pay_w, 110, begun)
+    features_others = gather_rep(pay, 112, moves)
+    weight_others.wait()
+    features_others.wait()
     for i in range(8):
-        grad_features[64 * i : 64 * i + 64, :] = pay[i, 0:64, :]
-        grad_weight[16 * i : 16 * i + 16, 0:128] = pay[i, 64:80, :]
-        grad_weight[16 * i : 16 * i + 16, 128:256] = pay[i, 80:96, :]
+        grad_features[64 * i : 64 * i + 64, :] = pay[i]
+        grad_weight[16 * i : 16 * i + 16, 0:128] = pay_w[i, 0:16, :]
+        grad_weight[16 * i : 16 * i + 16, 128:256] = pay_w[i, 16:32, :]
     out_move.wait()
     for copy in sent:
         copy.wait_send()
@@ -486,7 +502,8 @@
             vmem((4, 24, 256), F32),
             vmem((64, 128), F32),
             vmem((64, 128), F32),
-            vmem((8, 96, 128), F32),
+            vmem((8, 64, 128), F32),
+            vmem((8, 32, 128), F32),
             pltpu.SemaphoreType.DMA((12,)),
             pltpu.SemaphoreType.DMA((113,)),
             pltpu.SemaphoreType.DMA((113,)),

time: 74.8 us -> 74.4 us (level)
  no operation moved by 1% of the time
where the time goes in v6:
time: 74.4 us; the launch traced here: 74.3 us
  Pallas kernels  73 us (98%)
  between operations  1.29 us (2%)
    pallas_call x1, Pallas kernels, per_device(): pl.pallas_call(kernel, out_shape=shapes, in_specs=[hbm] * 8, out_specs=(h...  71 us
    pallas_call x1, Pallas kernels, per_device(): pl.pallas_call(finish_kernel, out_shape=shapes, in_specs=[hbm] * 4, out_s...  1.99 us

profile of v6, /device:TPU:1, one launch (start us, length us, event | category | flops | bytes accessed | tf_op | source)
XLA Modules:
  0.0 74.3 jit_solution(16090891475439647151)
XLA Ops:
  1.3 71.0 %shard_map.111 = (f32[512,256]{1,0:T(8,128)}, f32[512,128]{1,0:T(8,128)}, f32[128,256]{1,0:T(8,128)}, f32[1,256]{1,0:T(1,128)}) custom-call(s32[16]{0:T(128)} %rows_in.1, s32[16]{0:T(128)} %cols_in.1, s32[1]{0:T(128)S(6)} %copy.12.count_in, f32[8,64,128]{2,1,0:T(8,128)} %bitcast.3, f32[128,256]{1,0:T(8,128)} %weight_in.1, f32[1,256]{1,0:T(1,128)} %bitcast.4, ...), custom_call_target="tpu_custom_call" | custom-call | flops 400000000 | bytes 4000000 | tf_op jit(solution)/shard_map/pallas_call | solution.py:455
  72.3 2.0 %shard_map.112 = (f32[512,256]{1,0:T(8,128)}, f32[512,128]{1,0:T(8,128)}, f32[128,256]{1,0:T(8,128)}, f32[1,256]{1,0:T(1,128)}) custom-call(f32[512,256]{1,0:T(8,128)} %get-tuple-element.12.refs_0_, f32[512,128]{1,0:T(8,128)} %get-tuple-element.13.refs_1_, f32[128,256]{1,0:T(8,128)} %get-tuple-element.14.refs_2_, f32[1,256]{1,0:T(1,128)} %get-tuple-element.15.refs_3_), custom_call_target="tpu_custom_call" | custom-call | tf_op jit(solution)/shard_map/pallas_call | solution.py:527
